TPU v7x, 512 devices: a whole 4x4x16 slice. The times are simulated.
512 devices in a mesh: dp: 16 (over y, z_hi), seq: 32 (over z_lo, x, core).
Axes of the slice: x: 4, y: 4, z: 16 (z_hi: 4, z_lo: 4; z = z_hi * 4 + z_lo), core: 2. Of those that a mesh axis runs over, the one named last changes fastest.
Arguments:
- tokens: bfloat16 [1024, 64, 1152], P(('dp', 'seq')), may hold values from -6 to 6
- spatial_qkv: bfloat16 [1024, 64, 1728], P(('dp', 'seq')), may hold values from -6 to 6
- wo_spatial: bfloat16 [576, 1152], replicated, may hold values from -0.25 to 0.25
- w_temporal: bfloat16 [1152, 1728], P(None, 'dp'), may hold values from -0.1875 to 0.1875
- wo_temporal: bfloat16 [576, 1152], replicated, may hold values from -0.25 to 0.25
- cotangent: bfloat16 [1024, 64, 1152], P(('dp', 'seq')), may hold values from -24 to 24
Outputs:
- block_out: bfloat16 [1024, 64, 1152], P(('dp', 'seq'))
- tokens_grad: bfloat16 [1024, 64, 1152], P(('dp', 'seq'))
- spatial_qkv_grad: bfloat16 [1024, 64, 1728], P(('dp', 'seq'))
- wo_spatial_grad: float32 [576, 1152], P('seq', 'dp')
- wo_temporal_grad: float32 [576, 1152], P('seq', 'dp')
All inputs are finite; a program needn't handle non-finite values.
Results may differ from a plain program's by a relative error of at most 0.038.
Values may be sent and summed in bfloat16 or wider, within the bound.
A program may use at most 64 MiB of HBM per device.

v0:
```python
import math

import jax
import jax.numpy as jnp
from jax import lax
from jax.sharding import PartitionSpec as P

DH = 72
FRAMES = 16


def split_three(packed):
    inner_width = packed.shape[-1] // 3
    return (
        packed[..., :inner_width],
        packed[..., inner_width : 2 * inner_width],
        packed[..., 2 * inner_width :],
    )


def head_view(matrix):
    batch_size, length, inner_width = matrix.shape
    return matrix.reshape(batch_size, length, inner_width // DH, DH)


def attention_weights_of(query_heads, key_heads):
    scores = jnp.einsum(
        "blhd,bmhd->bhlm", query_heads, key_heads, preferred_element_type=jnp.float32
    ) * (1.0 / math.sqrt(DH))
    return jax.nn.softmax(scores, axis=-1)


def attention(queries, key_rows, values):
    batch_size, length, inner_width = queries.shape
    weights_full = attention_weights_of(head_view(queries), head_view(key_rows))
    rounded = weights_full.astype(jnp.bfloat16)
    output = jnp.einsum(
        "bhlm,bmhd->blhd", rounded, head_view(values), preferred_element_type=jnp.float32
    )
    return output.reshape(batch_size, length, inner_width).astype(jnp.bfloat16)


def attention_grad(queries, key_rows, values, output_grad):
    batch_size, length, inner_width = queries.shape
    query_heads = head_view(queries)
    key_heads = head_view(key_rows)
    value_heads = head_view(values)
    grad_heads = head_view(output_grad)
    weights_full = attention_weights_of(query_heads, key_heads)
    rounded = weights_full.astype(jnp.bfloat16)
    value_grad = jnp.einsum(
        "bhlm,blhd->bmhd", rounded, grad_heads, preferred_element_type=jnp.float32
    )
    weight_grad = jnp.einsum(
        "blhd,bmhd->bhlm", grad_heads, value_heads, preferred_element_type=jnp.float32
    )
    centered = weight_grad - jnp.sum(weights_full * weight_grad, axis=-1, keepdims=True)
    score_grad = (weights_full * centered * (1.0 / math.sqrt(DH))).astype(jnp.bfloat16)
    query_grad = jnp.einsum(
        "bhlm,bmhd->blhd", score_grad, key_heads, preferred_element_type=jnp.float32
    )
    key_grad = jnp.einsum(
        "bhlm,blhd->bmhd", score_grad, query_heads, preferred_element_type=jnp.float32
    )
    joined = [
        part_grad.reshape(batch_size, length, inner_width)
        for part_grad in (query_grad, key_grad, value_grad)
    ]
    return jnp.concatenate(joined, axis=-1).astype(jnp.bfloat16)


def to_clips(matrix, clip_count):
    frame_total, patch_share, channels = matrix.shape
    grouped = matrix.reshape(clip_count, FRAMES, patch_share, channels).transpose(0, 2, 1, 3)
    return grouped.reshape(clip_count * patch_share, FRAMES, channels)


def from_clips(matrix, clip_count):
    batch_rows, frame_count, channels = matrix.shape
    patch_share = batch_rows // clip_count
    grouped = matrix.reshape(clip_count, patch_share, frame_count, channels).transpose(0, 2, 1, 3)
    return grouped.reshape(clip_count * frame_count, patch_share, channels)


def times_transposed(left, right):
    return lax.dot_general(
        left, right, (((1,), (1,)), ((), ())), preferred_element_type=jnp.float32
    )


def transposed_times(left, right):
    return lax.dot_general(
        left, right, (((0,), (0,)), ((), ())), preferred_element_type=jnp.float32
    )


def forward_project(hidden_rows, weight_shard):
    return jnp.dot(
        hidden_rows,
        lax.all_gather(weight_shard, "dp", axis=1, tiled=True),
        preferred_element_type=jnp.float32,
    )


def backward_project(grad_rows, weight_shard):
    return times_transposed(grad_rows, lax.all_gather(weight_shard, "dp", axis=1, tiled=True))


def shards(tokens, spatial_qkv, wo_spatial, w_temporal, wo_temporal, cotangent):
    frames_dev, patches, feature_width = tokens.shape
    row_total = frames_dev * patches
    seq_devices = lax.axis_size("seq")
    clip_count = frames_dev * seq_devices // FRAMES
    spatial_query, spatial_keys, spatial_values = split_three(spatial_qkv)
    spatial_out = attention(spatial_query, spatial_keys, spatial_values)
    spatial_rows = spatial_out.reshape(row_total, -1)
    hidden_rows = (
        tokens.reshape(row_total, feature_width).astype(jnp.float32)
        + jnp.dot(spatial_rows, wo_spatial, preferred_element_type=jnp.float32)
    ).astype(jnp.bfloat16)
    frame_qkv = (
        forward_project(hidden_rows, w_temporal)
        .astype(jnp.bfloat16)
        .reshape(frames_dev, patches, -1)
    )
    patch_qkv = lax.all_to_all(frame_qkv, "seq", split_axis=1, concat_axis=0, tiled=True)
    temporal_query, temporal_keys, temporal_values = split_three(to_clips(patch_qkv, clip_count))
    patch_out = from_clips(attention(temporal_query, temporal_keys, temporal_values), clip_count)
    temporal_out = lax.all_to_all(patch_out, "seq", split_axis=0, concat_axis=1, tiled=True)
    temporal_rows = temporal_out.reshape(row_total, -1)
    block_out = (
        hidden_rows.astype(jnp.float32)
        + jnp.dot(temporal_rows, wo_temporal, preferred_element_type=jnp.float32)
    ).astype(jnp.bfloat16)
    grad_rows = cotangent.reshape(row_total, feature_width)
    out_grad = (
        times_transposed(grad_rows, wo_temporal)
        .astype(jnp.bfloat16)
        .reshape(frames_dev, patches, -1)
    )
    temporal_part = transposed_times(temporal_rows, grad_rows).astype(jnp.bfloat16)
    patch_out_grad = lax.all_to_all(out_grad, "seq", split_axis=1, concat_axis=0, tiled=True)
    clip_qkv_grad = attention_grad(
        temporal_query, temporal_keys, temporal_values, to_clips(patch_out_grad, clip_count)
    )
    patch_qkv_grad = from_clips(clip_qkv_grad, clip_count)
    frame_qkv_grad = lax.all_to_all(patch_qkv_grad, "seq", split_axis=0, concat_axis=1, tiled=True)
    projection_grad = backward_project(frame_qkv_grad.reshape(row_total, -1), w_temporal).astype(
        jnp.bfloat16
    )
    tokens_grad = (grad_rows.astype(jnp.float32) + projection_grad.astype(jnp.float32)).astype(
        jnp.bfloat16
    )
    spatial_out_grad = (
        times_transposed(tokens_grad, wo_spatial)
        .astype(jnp.bfloat16)
        .reshape(frames_dev, patches, -1)
    )
    spatial_part = transposed_times(spatial_rows, tokens_grad).astype(jnp.bfloat16)
    spatial_qkv_grad = attention_grad(spatial_query, spatial_keys, spatial_values, spatial_out_grad)
    seq_sums = (
        lax.psum_scatter(spatial_part, "seq", scatter_dimension=0, tiled=True).astype(jnp.float32),
        lax.psum_scatter(temporal_part, "seq", scatter_dimension=0, tiled=True).astype(jnp.float32),
    )
    spatial_weight_grad, temporal_weight_grad = (
        lax.psum_scatter(
            seq_sums[0].astype(jnp.bfloat16), "dp", scatter_dimension=1, tiled=True
        ).astype(jnp.float32),
        lax.psum_scatter(
            seq_sums[1].astype(jnp.bfloat16), "dp", scatter_dimension=1, tiled=True
        ).astype(jnp.float32),
    )
    return (
        block_out.reshape(frames_dev, patches, feature_width),
        tokens_grad.reshape(frames_dev, patches, feature_width),
        spatial_qkv_grad,
        spatial_weight_grad,
        temporal_weight_grad,
    )


def solution(mesh):
    placed = (
        P(("dp", "seq"), None, None),
        P(("dp", "seq"), None, None),
        P(),
        P(None, "dp"),
        P(),
        P(("dp", "seq"), None, None),
    )
    return jax.shard_map(
        shards,
        mesh=mesh,
        in_specs=placed,
        out_specs=(
            P(("dp", "seq"), None, None),
            P(("dp", "seq"), None, None),
            P(("dp", "seq"), None, None),
            P("seq", "dp"),
            P("seq", "dp"),
        ),
        check_vma=False,
    )
```

profile of v0, /device:TPU:1, one launch (start us, length us, event | category | flops | bytes accessed | tf_op | source)
XLA Modules:
  0.0 731.3 jit_solution(11731465842137330203)
XLA Ops:
  8.5 1.5 convolution_convert_fusion.13
  11.0 11.0 %all-to-all-start.2 = ((bf16[2,64,576]{2,0,1:T(2,128)(2,1)}), bf16[2,64,576]{2,0,1:T(2,128)(2,1)}, u32[]{:S(2)}, u32[]{:S(2)}) async-start(bf16[2,64,576]{2,0,1:T(2,128)(2,1)} %copy.76), calls=%async_computation.2 | async-start | bytes 327680 | tf_op jit(solution)/shard_map/all_to_all | solution.py:142
  24.3 2.4 fusion.21
  28.4 121.0 %all-gather.3.cloned.1.call-done = bf16[16,108,1152]{2,1,0:T(8,128)(2,1)} async-done(((bf16[1,108,1152]{2,1,0:T(8,128)(2,1)}), bf16[16,108,1152]{2,1,0:T(8,128)(2,1)}) %all-gather.3.cloned.1.call-update) | async-done | bytes 3981328 | tf_op jit(solution)/shard_map/all_gather | solution.py:100
  149.4 4.8 reshape.139
  154.2 4.1 convolution_convert_fusion.3
  160.8 6.0 all-to-all-start
  168.5 1.9 reshape_reshape.6
  170.3 11.5 %all-to-all-done = bf16[2,64,1728]{2,0,1:T(2,128)(2,1)S(1)} async-done(((bf16[2,64,1728]{2,0,1:T(2,128)(2,1)}), bf16[2,64,1728]{2,0,1:T(2,128)(2,1)S(1)}, u32[]{:S(2)}, u32[]{:S(2)}) %all-to-all-start) | async-done | bytes 442400 | tf_op jit(solution)/shard_map/all_to_all | solution.py:126
  183.0 1.9 reshape.123
  188.2 2.2 fusion.128
  190.4 2.3 fusion.22
  196.3 4.4 all-to-all-start.1
  200.7 2.2 fusion.25
  204.8 1.9 fusion.24
  207.6 2.0 fusion.23
  213.1 7.7 %all-to-all-start.3 = ((bf16[64,2,1728]{2,1,0:T(2,128)(2,1)}), bf16[64,2,1728]{2,1,0:T(2,128)(2,1)}, u32[]{:S(2)}, u32[]{:S(2)}) async-start(bf16[64,2,1728]{2,1,0:T(2,128)(2,1)} %copy.89), calls=%async_computation.3 | async-start | bytes 917504 | tf_op jit(solution)/shard_map/all_to_all | solution.py:147
  220.8 1.7 copy.198
  223.6 1.6 convolution_convert_fusion
  225.2 10.8 %all-to-all-done.3 = bf16[64,2,1728]{2,1,0:T(2,128)(2,1)} async-done(((bf16[64,2,1728]{2,1,0:T(2,128)(2,1)}), bf16[64,2,1728]{2,1,0:T(2,128)(2,1)}, u32[]{:S(2)}, u32[]{:S(2)}) %all-to-all-start.3) | async-done | bytes 442400 | tf_op jit(solution)/shard_map/all_to_all | solution.py:147
  235.9 2.1 copy.197
  238.0 2.2 reshape.132
  240.2 3.1 fusion.6
  243.3 1.6 convolution_convert_fusion.1
  245.0 1.3 dynamic-slice.2
  251.5 1.7 fusion.26
  253.6 274.9 %all-reduce.9.cloned.1.call-done = (bf16[576,1152]{1,0:T(8,128)(2,1)}, bf16[576,1152]{1,0:T(8,128)(2,1)}) async-done(((bf16[576,1152]{1,0:T(8,128)(2,1)}, bf16[576,1152]{1,0:T(8,128)(2,1)}), (bf16[576,1152]{1,0:T(8,128)(2,1)}, bf16[576,1152]{1,0:T(8,128)(2,1)})) %all-reduce.9.cloned.1.call-update) | async-done | bytes 2654224
  528.4 1.6 constant_dynamic-slice_fusion
  530.0 1.6 fusion.27
  533.8 188.3 %all-reduce.11.cloned.1.call-done = (bf16[18,1152]{1,0:T(8,128)(2,1)}, bf16[18,1152]{1,0:T(8,128)(2,1)}) async-done(((bf16[18,1152]{1,0:T(8,128)(2,1)}, bf16[18,1152]{1,0:T(8,128)(2,1)}), (bf16[18,1152]{1,0:T(8,128)(2,1)}, bf16[18,1152]{1,0:T(8,128)(2,1)})) %all-reduce.11.cloned.1.call-update) | async-done | bytes 82960
  722.0 1.4 dynamic-slice_convert_fusion.1
  723.4 1.4 dynamic-slice_convert_fusion
  (90 shorter events, 32.2 us)
Async XLA Ops:
  7.2 1.3 copy-start
  7.2 142.2 %all-gather.3.cloned.1.call-start = ((), (), s32[]{:S(2)}) async-start(), calls=%async_computation.4 | async-start | bytes 4386816 | tf_op jit(solution)/shard_map/all_gather | solution.py:100
  8.5 13.6 %copy-start.11 = (bf16[2,64,1728]{2,1,0:T(8,128)(2,1)S(1)}, bf16[2,64,1728]{2,1,0:T(8,128)(2,1)}, u32[]{:S(2)}) copy-start(bf16[2,64,1728]{2,1,0:T(8,128)(2,1)} %param.7) | copy-start | bytes 1327108
  11.0 149.7 %all-to-all-start.2 = ((bf16[2,64,576]{2,0,1:T(2,128)(2,1)}), bf16[2,64,576]{2,0,1:T(2,128)(2,1)}, u32[]{:S(2)}, u32[]{:S(2)}) async-start(bf16[2,64,576]{2,0,1:T(2,128)(2,1)} %copy.76), calls=%async_computation.2 | async-start | bytes 327680 | tf_op jit(solution)/shard_map/all_to_all | solution.py:142
  22.5 1.8 copy-start.13
  22.8 1.5 copy-start.15
  23.1 1.2 copy-start.8
  24.2 3.7 copy-start.1
  24.2 3.7 copy-start.12
  27.9 126.3 %copy-start.4 = (bf16[128,576]{1,0:T(8,128)(2,1)}, bf16[128,576]{1,0:T(8,128)(2,1)S(1)}, u32[]{:S(2)}) copy-start(bf16[128,576]{1,0:T(8,128)(2,1)S(1)} %convert_element_type.94) | copy-start | bytes 442372
  160.8 21.1 %all-to-all-start = ((bf16[2,64,1728]{2,0,1:T(2,128)(2,1)}), bf16[2,64,1728]{2,0,1:T(2,128)(2,1)S(1)}, u32[]{:S(2)}, u32[]{:S(2)}) async-start(bf16[2,64,1728]{2,0,1:T(2,128)(2,1)} %copy.64), calls=%async_computation | async-start | bytes 917504 | tf_op jit(solution)/shard_map/all_to_all | solution.py:126
  182.3 4.9 copy-start.10
  196.3 16.8 %all-to-all-start.1 = ((bf16[64,2,576]{2,1,0:T(2,128)(2,1)}), bf16[64,2,576]{2,1,0:T(2,128)(2,1)}, u32[]{:S(2)}, u32[]{:S(2)}) async-start(bf16[64,2,576]{2,1,0:T(2,128)(2,1)} %copy.73), calls=%async_computation.1 | async-start | bytes 327680 | tf_op jit(solution)/shard_map/all_to_all | solution.py:129
  211.8 11.7 %copy-start.2 = (bf16[2,64,1152]{2,1,0:T(8,128)(2,1)S(1)}, bf16[2,64,1152]{2,1,0:T(8,128)(2,1)}, u32[]{:S(2)}) copy-start(bf16[2,64,1152]{2,1,0:T(8,128)(2,1)} %param.11) | copy-start | bytes 884740
  213.1 22.8 %all-to-all-start.3 = ((bf16[64,2,1728]{2,1,0:T(2,128)(2,1)}), bf16[64,2,1728]{2,1,0:T(2,128)(2,1)}, u32[]{:S(2)}, u32[]{:S(2)}) async-start(bf16[64,2,1728]{2,1,0:T(2,128)(2,1)} %copy.89), calls=%async_computation.3 | async-start | bytes 917504 | tf_op jit(solution)/shard_map/all_to_all | solution.py:147
  220.8 307.7 %all-reduce.9.cloned.1.call-start = ((), (), s32[]{:S(2)}) async-start(), calls=%async_computation.5 | async-start | bytes 5308416
  223.6 14.5 %copy-start.6 = (bf16[128,576]{1,0:T(8,128)(2,1)}, bf16[128,576]{1,0:T(8,128)(2,1)S(1)}, u32[]{:S(2)}) copy-start(bf16[128,576]{1,0:T(8,128)(2,1)S(1)} %reshape.126) | copy-start | bytes 442372
  240.2 3.1 copy-start.5
  243.3 6.7 copy-start.3
  244.9 3.9 copy-start.7
  245.0 477.1 %all-reduce.11.cloned.1.call-start = ((), (), s32[]{:S(2)}) async-start(), calls=%async_computation.6 | async-start | bytes 221184
  250.0 1.0 copy-start.9
  250.5 1.0 copy-start.16
  251.5 1.7 copy-start.14
Sparse Core Ops, SparseCore 0:
  11.1 138.2 all-gather.2
  245.1 283.2 all-reduce.8
  531.4 190.5 all-reduce.10
where the time goes:
time: 742 us; the launch traced here: 731 us
  waiting for transfers between devices  607 us (82%)
  local copies, waits for them, and re-layouts  43.8 us (6%)
  matrix products  33.1 us (4%)
  starting transfers between devices  29.1 us (4%)
  between operations  15.5 us (2%)
    unnamed x5, waiting for transfers between devices  464 us
    all_gather x1, waiting for transfers between devices, forward_project(): lax.all_gather(weight_shard, 'dp', axis=1, tiled=True)  121 us
  transfers between devices with their start and end apart: 7, of which 5 were waited for; matrix products, arithmetic and copies ran while one was open for 7% of the time, Pallas kernels for 0%

commit v1 on v0

v1 whole, which is shorter than its diff:
```python
import functools
import math

import jax
import jax.numpy as jnp
from jax import lax
from jax.experimental import pallas as pl
from jax.experimental.pallas import tpu as pltpu
from jax.sharding import PartitionSpec as P

DH = 72
FRAMES = 16
MESH = pl.DeviceIdType.MESH
VMEM_LIMIT = 60 * 1024 * 1024


def coords():
    dp, seq = lax.axis_index("dp"), lax.axis_index("seq")
    return dp // 4, dp % 4, seq // 8, (seq // 2) % 4, seq % 2


def device(y, zh, zl, x, core):
    return (y * 4 + zh, (zl * 4 + x) * 2 + core)


def greet(partners):
    barrier = pltpu.get_barrier_semaphore()
    for partner in partners:
        pl.semaphore_signal(barrier, inc=1, device_id=partner, device_id_type=MESH)
    pl.semaphore_wait(barrier, len(partners))


def remote(src, dst, send_sem, recv_sem, target):
    return pltpu.make_async_remote_copy(
        src_ref=src, dst_ref=dst, send_sem=send_sem, recv_sem=recv_sem,
        device_id=target, device_id_type=MESH,
    )


def gather_kernel(w_ref, out_ref, own_sem, zs, zr, fs, fr, ss, sr, ps, pr):
    y, zh, zl, x, c = coords()
    rows = w_ref.shape[0] // 8
    u = (1 - c) * y + c * x
    v = (1 - c) * x + c * y

    def at(u_, v_):
        y_ = (1 - c) * u_ + c * v_
        x_ = (1 - c) * v_ + c * u_
        return device(y_, zh, zl, x_, c)

    firsts = [at((u + d) % 4, v) for d in range(1, 4)]
    seconds = [at(u, (v + d) % 4) for d in range(1, 4)]
    zs_to = [device(y, (zh + d) % 4, zl, x, c) for d in range(1, 4)]
    partner = device(y, zh, zl, x, 1 - c)
    greet(firsts + seconds + zs_to + [partner])

    piece = w_ref.at[pl.ds((c * 4 + x) * rows, rows)]
    mine = out_ref.at[zh, c, v, u]
    own = pltpu.make_async_copy(piece, mine, own_sem)
    own.start()
    pending = []

    def send(copy):
        copy.start()
        pending.append(copy)

    zcopies = {}
    for d in (1, 3, 2):
        zcopies[d] = remote(piece, mine, zs.at[d - 1], zr.at[d - 1], zs_to[d - 1])
        send(zcopies[d])
    own.wait()
    order = (0, 1, 3, 2)
    first, second, cross = {}, {}, {}
    for step in range(6):
        if step < 4:
            e = order[step]
            zset = (zh + 4 - e) % 4
            if e:
                zcopies[e].wait_recv()
            for d in range(1, 4):
                ref = out_ref.at[zset, c, v, u]
                first[e, d] = remote(ref, ref, fs.at[e, d - 1], fr.at[e, d - 1], firsts[d - 1])
                send(first[e, d])
        if 1 <= step < 5:
            e = order[step - 1]
            zset = (zh + 4 - e) % 4
            for d in range(1, 4):
                first[e, d].wait_recv()
            ref = out_ref.at[zset, c, v]
            for d in range(1, 4):
                second[e, d] = remote(ref, ref, ss.at[e, d - 1], sr.at[e, d - 1], seconds[d - 1])
                send(second[e, d])
            cross[e, 0] = remote(ref, ref, ps.at[e, 0], pr.at[e, 0], partner)
            send(cross[e, 0])
        if step >= 2:
            e = order[step - 2]
            zset = (zh + 4 - e) % 4
            for d in range(1, 4):
                second[e, d].wait_recv()
                ref = out_ref.at[zset, c, (v + 4 - d) % 4]
                cross[e, d] = remote(ref, ref, ps.at[e, d], pr.at[e, d], partner)
                send(cross[e, d])
    for e in range(4):
        for d in range(4):
            cross[e, d].wait_recv()
    for copy in pending:
        copy.wait_send()


def gather_weights(w_shard):
    depth = w_shard.shape[0]
    padded = jnp.pad(w_shard, ((0, 0), (0, 128 - w_shard.shape[1])))
    sems = pltpu.SemaphoreType.DMA
    gathered = pl.pallas_call(
        gather_kernel,
        out_shape=jax.ShapeDtypeStruct((4, 2, 4, 4, depth // 8, 128), jnp.bfloat16),
        in_specs=[pl.BlockSpec(memory_space=pltpu.VMEM)],
        out_specs=pl.BlockSpec(memory_space=pltpu.VMEM),
        scratch_shapes=[
            sems, sems((3,)), sems((3,)), sems((4, 3)), sems((4, 3)), sems((4, 3)), sems((4, 3)),
            sems((4, 4)), sems((4, 4)),
        ],
        compiler_params=pltpu.CompilerParams(
            collective_id=0, has_side_effects=True, vmem_limit_bytes=VMEM_LIMIT
        ),
        name="gather_weights",
    )(padded)
    return gathered


def whole_weights(gathered, width):
    zh, _, _, _, rows, lanes = gathered.shape
    upper = gathered[:, 0].transpose(1, 3, 2, 0, 4)
    lower = gathered[:, 1].transpose(2, 3, 1, 0, 4)
    both = jnp.stack([upper, lower])[..., :width]
    return both.reshape(8 * rows, 16 * width)


def exchange_kernel(count, *refs):
    srcs, dsts = refs[:count], refs[count : 2 * count]
    own_sem, send_sems, recv_sems = refs[2 * count :]
    y, zh, zl, x, c = coords()
    me = x * 2 + c
    others = [(me + d) % 8 for d in range(1, 8)]
    ids = [device(y, zh, zl, j // 2, j % 2) for j in others]
    greet(ids)
    copies = []
    for k in range(count):
        for n, d in enumerate((1, 7, 2, 6, 3, 5, 4)):
            copies.append(
                remote(
                    srcs[k].at[others[d - 1]], dsts[k].at[me], send_sems.at[k, d - 1],
                    recv_sems.at[k, d - 1], ids[d - 1],
                )
            )
            copies[-1].start()
    for k in range(count):
        own = pltpu.make_async_copy(srcs[k].at[me], dsts[k].at[me], own_sem)
        own.start()
        own.wait()
    for copy in copies:
        copy.wait()


def exchange(collective_id, *arrays):
    count = len(arrays)
    vmem = pl.BlockSpec(memory_space=pltpu.VMEM)
    sems = pltpu.SemaphoreType.DMA
    return pl.pallas_call(
        functools.partial(exchange_kernel, count),
        out_shape=[jax.ShapeDtypeStruct(a.shape, a.dtype) for a in arrays],
        in_specs=[vmem] * count,
        out_specs=[vmem] * count,
        scratch_shapes=[sems, sems((count, 7)), sems((count, 7))],
        compiler_params=pltpu.CompilerParams(
            collective_id=collective_id, has_side_effects=True, vmem_limit_bytes=VMEM_LIMIT
        ),
        name=f"exchange_{collective_id}",
    )(*arrays)


def sum_kernel(
    lt_ref, r_ref, out_ref, ltx, rx, xs, xr, ysend, yrecv, zsend, zrecv,
    os_, or_, xss, xrs, yss, yrs, zss, zrs,
):
    y, zh, zl, x, c = coords()
    weights = lt_ref.shape[0]
    partner = device(y, zh, zl, x, 1 - c)
    xs_to = [device(y, zh, zl, (x + d) % 4, c) for d in range(1, 4)]
    ys_to = [device((y + d) % 4, zh, zl, x, c) for d in range(1, 4)]
    zpos = zh * 4 + zl
    z_at = [(zpos + d) % 16 for d in range(1, 16)]
    zs_to = [device(y, z // 4, z % 4, x, c) for z in z_at]
    greet([partner] + xs_to + ys_to + zs_to)
    swaps = []
    for w in range(weights):
        pair = (
            remote(lt_ref.at[w, 1 - c], ltx.at[w], os_.at[w, 0], or_.at[w, 0], partner),
            remote(r_ref.at[w], rx.at[w], os_.at[w, 1], or_.at[w, 1], partner),
        )
        for copy in pair:
            copy.start()
        swaps.append(pair)
    done = []
    xcopies = []
    for w in range(weights):
        for copy in swaps[w]:
            copy.wait()
        left, right = lt_ref[w, c], r_ref[w]
        for k in range(4):
            rows = slice(k * 80, (k + 1) * 80)
            total = jnp.dot(left[rows], right, preferred_element_type=jnp.float32) + jnp.dot(
                ltx[w, rows], rx[w], preferred_element_type=jnp.float32
            )
            xs[w, k] = total.astype(jnp.bfloat16)
        row = []
        for d in (1, 3, 2):
            row.append(
                remote(xs.at[w, (x + d) % 4], xr.at[w, d - 1], xss.at[w, d - 1], xrs.at[w, d - 1], xs_to[d - 1])
            )
            row[-1].start()
        xcopies.append(row)
    ycopies = []
    for w in range(weights):
        for copy in xcopies[w]:
            copy.wait()
        total = xs[w, x].astype(jnp.float32)
        for d in range(3):
            total += xr[w, d].astype(jnp.float32)
        for k in range(4):
            ysend[w, k, :, 0:288] = total[:, k * 288 : (k + 1) * 288].astype(jnp.bfloat16)
        row = []
        for d in (1, 3, 2):
            row.append(
                remote(ysend.at[w, (y + d) % 4], yrecv.at[w, d - 1], yss.at[w, d - 1], yrs.at[w, d - 1], ys_to[d - 1])
            )
            row[-1].start()
        ycopies.append(row)
    zcopies = []
    for w in range(weights):
        for copy in ycopies[w]:
            copy.wait()
        total = ysend[w, y].astype(jnp.float32)
        for d in range(3):
            total += yrecv[w, d].astype(jnp.float32)
        for zh_ in range(4):
            for zl_ in range(4):
                zsend[w, zh_ * 4 + zl_, 0:18, 0:72] = total[
                    zl_ * 18 : (zl_ + 1) * 18, zh_ * 72 : (zh_ + 1) * 72
                ]
        row = []
        for d in range(1, 16):
            row.append(
                remote(
                    zsend.at[w, z_at[d - 1]], zrecv.at[w, d - 1], zss.at[w, d - 1], zrs.at[w, d - 1], zs_to[d - 1]
                )
            )
            row[-1].start()
        zcopies.append(row)
    for w in range(weights):
        total = zsend[w, zpos]
        for d in range(15):
            zcopies[w][d].wait()
            total += zrecv[w, d]
        out_ref[w] = total


def weight_sums(lefts, rights):
    weights, rows, inner = lefts.shape
    width = rights.shape[-1]
    by_core = lefts.reshape(weights, rows, 4, 4, 2, 18).transpose(0, 4, 3, 2, 5, 1)
    by_core = by_core.reshape(weights, 2, 4, 72, rows)
    by_core = jnp.pad(by_core, ((0, 0), (0, 0), (0, 0), (0, 8), (0, 0)))
    by_core = by_core.reshape(weights, 2, 320, rows)
    vmem = pl.BlockSpec(memory_space=pltpu.VMEM)
    sems = pltpu.SemaphoreType.DMA
    bf, f32 = jnp.bfloat16, jnp.float32
    out = pl.pallas_call(
        sum_kernel,
        out_shape=jax.ShapeDtypeStruct((weights, 24, 128), f32),
        in_specs=[vmem, vmem],
        out_specs=vmem,
        scratch_shapes=[
            pltpu.VMEM((weights, 320, rows), bf),
            pltpu.VMEM((weights, rows, width), bf),
            pltpu.VMEM((weights, 4, 80, width), bf),
            pltpu.VMEM((weights, 3, 80, width), bf),
            pltpu.VMEM((weights, 4, 80, 384), bf),
            pltpu.VMEM((weights, 3, 80, 384), bf),
            pltpu.VMEM((weights, 16, 24, 128), f32),
            pltpu.VMEM((weights, 15, 24, 128), f32),
            sems((weights, 2)), sems((weights, 2)),
            sems((weights, 3)), sems((weights, 3)),
            sems((weights, 3)), sems((weights, 3)),
            sems((weights, 15)), sems((weights, 15)),
        ],
        compiler_params=pltpu.CompilerParams(
            collective_id=9, has_side_effects=True, vmem_limit_bytes=VMEM_LIMIT
        ),
        name="weight_sums",
    )(by_core, rights)
    return out[:, :18, :72]


def split_three(packed):
    inner_width = packed.shape[-1] // 3
    return (
        packed[..., :inner_width],
        packed[..., inner_width : 2 * inner_width],
        packed[..., 2 * inner_width :],
    )


def head_view(matrix):
    batch_size, length, inner_width = matrix.shape
    return matrix.reshape(batch_size, length, inner_width // DH, DH)


def attention_weights_of(query_heads, key_heads):
    scores = jnp.einsum(
        "blhd,bmhd->bhlm", query_heads, key_heads, preferred_element_type=jnp.float32
    ) * (1.0 / math.sqrt(DH))
    return jax.nn.softmax(scores, axis=-1)


def attention(queries, key_rows, values):
    batch_size, length, inner_width = queries.shape
    weights_full = attention_weights_of(head_view(queries), head_view(key_rows))
    rounded = weights_full.astype(jnp.bfloat16)
    output = jnp.einsum(
        "bhlm,bmhd->blhd", rounded, head_view(values), preferred_element_type=jnp.float32
    )
    return output.reshape(batch_size, length, inner_width).astype(jnp.bfloat16)


def attention_grad(queries, key_rows, values, output_grad):
    batch_size, length, inner_width = queries.shape
    query_heads = head_view(queries)
    key_heads = head_view(key_rows)
    value_heads = head_view(values)
    grad_heads = head_view(output_grad)
    weights_full = attention_weights_of(query_heads, key_heads)
    rounded = weights_full.astype(jnp.bfloat16)
    value_grad = jnp.einsum(
        "bhlm,blhd->bmhd", rounded, grad_heads, preferred_element_type=jnp.float32
    )
    weight_grad = jnp.einsum(
        "blhd,bmhd->bhlm", grad_heads, value_heads, preferred_element_type=jnp.float32
    )
    centered = weight_grad - jnp.sum(weights_full * weight_grad, axis=-1, keepdims=True)
    score_grad = (weights_full * centered * (1.0 / math.sqrt(DH))).astype(jnp.bfloat16)
    query_grad = jnp.einsum(
        "bhlm,bmhd->blhd", score_grad, key_heads, preferred_element_type=jnp.float32
    )
    key_grad = jnp.einsum(
        "bhlm,blhd->bmhd", score_grad, query_heads, preferred_element_type=jnp.float32
    )
    joined = [
        part_grad.reshape(batch_size, length, inner_width)
        for part_grad in (query_grad, key_grad, value_grad)
    ]
    return jnp.concatenate(joined, axis=-1).astype(jnp.bfloat16)


def times_transposed(left, right):
    return lax.dot_general(
        left, right, (((1,), (1,)), ((), ())), preferred_element_type=jnp.float32
    )


def by_peer(matrix):
    frames, patches, width = matrix.shape
    return matrix.reshape(frames, 8, patches // 8, width).transpose(1, 0, 2, 3).reshape(8, -1, width)


def from_peer(blocks, frames):
    peers, rows, width = blocks.shape
    return (
        blocks.reshape(peers, frames, rows // frames, width)
        .transpose(1, 0, 2, 3)
        .reshape(frames * peers * rows // frames, width)
    )


def clip_rows(blocks, frames):
    peers, rows, width = blocks.shape
    return (
        blocks.reshape(peers, frames, rows // frames, width)
        .transpose(2, 0, 1, 3)
        .reshape(rows // frames, peers * frames, width)
    )


def peer_blocks(rows, frames):
    patches, total, width = rows.shape
    return (
        rows.reshape(patches, total // frames, frames, width)
        .transpose(1, 2, 0, 3)
        .reshape(total // frames, frames * patches, width)
    )


def shards(tokens, spatial_qkv, wo_spatial, w_temporal, wo_temporal, cotangent):
    frames_dev, patches, feature_width = tokens.shape
    row_total = frames_dev * patches
    width = w_temporal.shape[1]
    weights = whole_weights(gather_weights(w_temporal), width)
    spatial_query, spatial_keys, spatial_values = split_three(spatial_qkv)
    spatial_out = attention(spatial_query, spatial_keys, spatial_values)
    spatial_rows = spatial_out.reshape(row_total, -1)
    hidden_rows = (
        tokens.reshape(row_total, feature_width).astype(jnp.float32)
        + jnp.dot(spatial_rows, wo_spatial, preferred_element_type=jnp.float32)
    ).astype(jnp.bfloat16)
    grad_rows = cotangent.reshape(row_total, feature_width)
    out_grad = times_transposed(grad_rows, wo_temporal).astype(jnp.bfloat16)
    hidden_p, out_grad_p = exchange(
        1,
        by_peer(hidden_rows.reshape(frames_dev, patches, -1)),
        by_peer(out_grad.reshape(frames_dev, patches, -1)),
    )
    hidden_clip = clip_rows(hidden_p, frames_dev)
    qkv = jnp.dot(
        hidden_clip.reshape(row_total, -1), weights, preferred_element_type=jnp.float32
    ).astype(jnp.bfloat16)
    qkv = qkv.reshape(8, FRAMES, -1)
    temporal_query, temporal_keys, temporal_values = split_three(qkv)
    temporal_clip = attention(temporal_query, temporal_keys, temporal_values)
    qkv_grad = attention_grad(
        temporal_query, temporal_keys, temporal_values, clip_rows(out_grad_p, frames_dev)
    )
    projection_clip = times_transposed(qkv_grad.reshape(row_total, -1), weights).astype(jnp.bfloat16)
    projection_p, temporal_p = exchange(
        2,
        peer_blocks(projection_clip.reshape(8, FRAMES, -1), frames_dev),
        peer_blocks(temporal_clip, frames_dev),
    )
    projection_grad = from_peer(projection_p, frames_dev)
    temporal_rows = from_peer(temporal_p, frames_dev)
    block_out = (
        hidden_rows.astype(jnp.float32)
        + jnp.dot(temporal_rows, wo_temporal, preferred_element_type=jnp.float32)
    ).astype(jnp.bfloat16)
    tokens_grad = (grad_rows.astype(jnp.float32) + projection_grad.astype(jnp.float32)).astype(
        jnp.bfloat16
    )
    spatial_out_grad = (
        times_transposed(tokens_grad, wo_spatial)
        .astype(jnp.bfloat16)
        .reshape(frames_dev, patches, -1)
    )
    spatial_qkv_grad = attention_grad(spatial_query, spatial_keys, spatial_values, spatial_out_grad)
    sums = weight_sums(
        jnp.stack([spatial_rows, temporal_rows]), jnp.stack([tokens_grad, grad_rows])
    )
    return (
        block_out.reshape(frames_dev, patches, feature_width),
        tokens_grad.reshape(frames_dev, patches, feature_width),
        spatial_qkv_grad,
        sums[0],
        sums[1],
    )


def solution(mesh):
    placed = (
        P(("dp", "seq"), None, None),
        P(("dp", "seq"), None, None),
        P(),
        P(None, "dp"),
        P(),
        P(("dp", "seq"), None, None),
    )
    return jax.shard_map(
        shards,
        mesh=mesh,
        in_specs=placed,
        out_specs=(
            P(("dp", "seq"), None, None),
            P(("dp", "seq"), None, None),
            P(("dp", "seq"), None, None),
            P("seq", "dp"),
            P("seq", "dp"),
        ),
        check_vma=False,
    )
```

time: 742 us -> 255 us (0.34); the launches traced: 731 us -> 253 us
  waiting for transfers between devices: 607 us -> 0 us
  Pallas kernels: 0 us -> 124 us
  local copies, waits for them, and re-layouts: 43.8 us -> 84.8 us
  starting transfers between devices: 29.1 us -> 0 us
  between operations: 15.5 us -> 0.93 us
    unnamed x5 -> x0, waiting for transfers between devices: 464 us -> none
    pallas_call x0 -> x4, Pallas kernels: none -> 124 us  [the longest x1 53.5 us: weight_sums(): pl.pallas_call(sum_kernel, out_shape=jax.ShapeDtypeStruct((weights, 24, 1...]
    all_gather x1 -> x0, waiting for transfers between devices: 121 us -> none  [forward_project(): lax.all_gather(weight_shard, 'dp', axis=1, tiled=True)]
    all_to_all x4 -> x0, starting transfers between devices: 29 us -> none  [the longest x1 11 us: shards(): lax.all_to_all(out_grad, 'seq', split_axis=1, concat_axis=0, tiled=True)]
    all_to_all x4 -> x0, waiting for transfers between devices: 22.3 us -> none  [the longest x1 11.5 us: shards(): lax.all_to_all(frame_qkv, 'seq', split_axis=1, concat_axis=0, tiled=True)]
    another operation x0 -> x6, local copies, waits for them, and re-layouts: none -> 11.5 us  [the longest x2 7.15 us: shards(): jnp.stack([spatial_rows, temporal_rows])]
    slice x0 -> x2, local copies, waits for them, and re-layouts: none -> 8.46 us  [the longest x1 5.77 us: whole_weights(): both = jnp.stack([upper, lower])[..., :width]]
  transfers between devices with their start and end apart: 7 -> 0, of which waited for: 5 -> 0; matrix products, arithmetic and copies ran while one was open for 7% -> 0% of each run, Pallas kernels for 0% -> 0%
where the time goes in v1:
time: 255 us; the launch traced here: 253 us
  Pallas kernels  124 us (49%)
  local copies, waits for them, and re-layouts  84.8 us (33%)
  matrix products  39.9 us (16%)
  other arithmetic  3.36 us (1%)
    pallas_call x1, Pallas kernels, weight_sums(): pl.pallas_call(sum_kernel, out_shape=jax.ShapeDtypeStruct((weights, 24, 1...  53.5 us
    pallas_call x1, Pallas kernels, gather_weights(): pl.pallas_call(gather_kernel, out_shape=jax.ShapeDtypeStruct((4, 2, 4, 4,...  40.3 us
    pallas_call x2, Pallas kernels, exchange(): pl.pallas_call(functools.partial(exchange_kernel, count), out_shape=[jax....  30 us
    reshape x1, local copies, waits for them, and re-layouts, whole_weights(): return both.reshape(8 * rows, 16 * width)  8.85 us
    another operation x2, local copies, waits for them, and re-layouts, shards(): jnp.stack([spatial_rows, temporal_rows])  7.15 us
    convert_element_type x6, local copies, waits for them, and re-layouts, attention(): return output.reshape(batch_size, length, inner_width).astype(jnp.bfloat16)  6.63 us
    concatenate x5, local copies, waits for them, and re-layouts, attention_grad(): return jnp.concatenate(joined, axis=-1).astype(jnp.bfloat16)  6.57 us
    dot_general x3, matrix products, times_transposed(): lax.dot_general(left, right, (((1,), (1,)), ((), ())), preferred_element_...  6.07 us

profile of v1, /device:TPU:1, one launch (start us, length us, event | category | flops | bytes accessed | tf_op | source)
XLA Modules:
  0.0 252.8 jit_solution(7345073484980558058)
XLA Ops:
  11.7 18.1 %exchange_1.1 = (bf16[8,16,1152]{2,1,0:T(8,128)(2,1)}, bf16[8,16,576]{2,1,0:T(8,128)(2,1)}) custom-call(bf16[8,16,1152]{2,1,0:T(8,128)(2,1)} %bitcast.147, bf16[8,16,576]{2,1,0:T(8,128)(2,1)} %bitcast.153), custom_call_target="tpu_custom_call" | custom-call | tf_op jit(solution)/shard_map/exchange_1/pallas_call | solution.py:169
  29.8 1.9 copy.169
  36.4 40.3 %gather_weights.1 = bf16[4,2,4,4,144,128]{5,4,3,2,1,0:T(8,128)(2,1)} custom-call(bf16[1152,128]{1,0:T(8,128)(2,1)} %pad.8.w_ref), custom_call_target="tpu_custom_call" | custom-call | tf_op jit(solution)/shard_map/gather_weights/pallas_call | solution.py:114
  76.7 2.7 %fusion.120 = (bf16[4,1,4,4,144,128]{5,4,3,2,1,0:T(8,128)(2,1)S(1)}, bf16[1,4,144,4,4,128]{5,2,1,3,4,0:T(8,128)(2,1)S(1)}) fusion(bf16[4,2,4,4,144,128]{5,4,3,2,1,0:T(8,128)(2,1)} %gather_weights.1), kind=kLoop, calls=%fused_computation.104 | loop fusion | bytes 9437184 | tf_op jit(solution)/shard_map/slice | solution.py:133
  80.1 5.8 %copy.34 = bf16[2,4,144,4,4,108]{5,4,3,2,1,0:T(4,128)(2,1)} copy(bf16[2,4,144,4,4,108]{5,2,1,3,4,0:T(8,128)(2,1)S(1)} %pad_maximum_fusion) | data formatting | bytes 7962624 | tf_op jit(solution)/shard_map/slice | solution.py:135
  85.9 8.9 %reshape.185 = bf16[1152,1728]{1,0:T(8,128)(2,1)} reshape(bf16[2,4,144,4,4,108]{5,4,3,2,1,0:T(4,128)(2,1)} %copy.34) | data formatting | bytes 7962624 | tf_op jit(solution)/shard_map/reshape | solution.py:136
  94.7 4.6 %convolution_convert_fusion.1 = bf16[128,1728]{0,1:T(8,128)(2,1)} fusion(bf16[128,1152]{1,0:T(8,128)(2,1)S(1)} %reshape_reshape.20, bf16[1152,1728]{1,0:T(8,128)(2,1)} %reshape.185), kind=kOutput, calls=%fused_computation.10 | convolution fusion | flops 509829120 | bytes 4718592 | tf_op jit(solution)/shard_map/dot_general | solution.py:423
  99.3 2.0 copy.35
  101.3 1.9 fusion.121
  103.2 1.9 reshape.187
  106.1 2.2 fusion.128
  110.2 2.3 fusion.22
  116.2 2.3 fusion.21
  120.4 2.1 fusion.43
  122.5 2.6 %fusion.20 = bf16[8,16,8,72]{3,1,2,0:T(8,128)(2,1)} fusion(f32[8,8,16,16]{2,3,1,0:T(8,128)} %fusion.43, bf16[8,16,8,72]{3,2,1,0:T(8,128)(2,1)} %reshape.188, f32[8,8,16,16]{2,3,1,0:T(8,128)} %get-tuple-element.28, f32[8,8,16]{2,1,0:T(8,128)S(1)} %get-tuple-element.27), kind=kOutput, calls=%fused_computation.37 | convolution fusion | flops 2548751 | bytes 430080 | tf_op jit(solution)/shard_map/bhlm,blhd->bmhd/dot_general | solution.py:355
  127.0 2.8 %fusion.19 = bf16[8,16,8,72]{3,1,2,0:T(8,128)(2,1)} fusion(f32[8,8,16,16]{2,3,1,0:T(8,128)} %fusion.43, bf16[8,16,8,72]{3,2,1,0:T(8,128)(2,1)} %reshape.187, f32[8,8,16,16]{2,3,1,0:T(8,128)} %get-tuple-element.28, f32[8,8,16]{2,1,0:T(8,128)S(1)} %get-tuple-element.27), kind=kOutput, calls=%fused_computation.36 | convolution fusion | flops 2548751 | bytes 430080 | tf_op jit(solution)/shard_map/bhlm,bmhd->blhd/dot_general | solution.py:352
  131.7 2.0 concatenate.19
  133.7 3.7 %convolution_convert_fusion = bf16[128,1152]{1,0:T(8,128)(2,1)S(1)} fusion(bf16[128,1728]{1,0:T(8,128)(2,1)} %concatenate.19, bf16[1152,1728]{1,0:T(8,128)(2,1)} %reshape.185), kind=kOutput, calls=%fused_computation.9 | convolution fusion | flops 509755392 | bytes 4718592 | tf_op jit(solution)/shard_map/dot_general | solution.py:366
  140.0 11.9 %exchange_2.1 = (bf16[8,16,1152]{2,1,0:T(8,128)(2,1)}, bf16[8,16,576]{2,1,0:T(8,128)(2,1)}) custom-call(bf16[8,16,1152]{2,1,0:T(8,128)(2,1)} %bitcast.148, bf16[8,16,576]{2,1,0:T(8,128)(2,1)} %bitcast.152), custom_call_target="tpu_custom_call" | custom-call | tf_op jit(solution)/shard_map/exchange_2/pallas_call | solution.py:169
  153.5 3.5 %stack.21 = bf16[1,128,4,4,2,18]{5,4,3,2,1,0:T(2,128)(2,1)} reshape(bf16[2,8,8,576]{3,2,1,0:T(8,128)(2,1)S(1)} %get-tuple-element.21) | data formatting | bytes 294912 | tf_op jit(solution)/shard_map/stack | solution.py:454
  157.0 3.6 %copy.64 = bf16[1,128,4,4,2,18]{1,5,4,3,2,0:T(8,128)(2,1)} copy(bf16[1,128,4,4,2,18]{5,4,3,2,1,0:T(2,128)(2,1)} %stack.21) | data formatting | bytes 294912 | tf_op jit(solution)/shard_map/stack | solution.py:454
  162.5 1.9 convert_element_type.173
  167.4 53.5 %weight_sums.1 = f32[2,24,128]{2,1,0:T(8,128)} custom-call(bf16[2,2,320,128]{3,2,1,0:T(8,128)(2,1)} %bitcast.146, bf16[2,128,1152]{2,1,0:T(8,128)(2,1)} %pad_maximum_fusion.1.r_ref), custom_call_target="tpu_custom_call" | custom-call | tf_op jit(solution)/shard_map/weight_sums/pallas_call | solution.py:278
  227.1 2.2 fusion.25
  231.1 1.9 reshape.198
  233.0 2.1 fusion.49
  235.1 2.7 %fusion.24 = bf16[2,64,8,72]{3,1,2,0:T(8,128)(2,1)} fusion(f32[2,8,64,64]{2,3,1,0:T(8,128)} %fusion.49, bf16[2,64,8,72]{3,2,1,0:T(8,128)(2,1)} %copy-done.9, f32[2,8,64,64]{2,3,1,0:T(8,128)} %get-tuple-element.26, f32[2,8,64]{2,1,0:T(8,128)S(1)} %copy-done.11), kind=kOutput, calls=%fused_computation.41 | convolution fusion | flops 9970751 | bytes 823296 | tf_op jit(solution)/shard_map/bhlm,blhd->bmhd/dot_general | solution.py:355
  239.6 1.9 reshape.197
  241.5 2.8 %fusion.23 = bf16[2,64,8,72]{3,1,2,0:T(8,128)(2,1)} fusion(f32[2,8,64,64]{2,3,1,0:T(8,128)} %fusion.49, bf16[2,64,8,72]{3,2,1,0:T(8,128)(2,1)} %copy-done.8, f32[2,8,64,64]{2,3,1,0:T(8,128)} %get-tuple-element.26, f32[2,8,64]{2,1,0:T(8,128)S(1)} %copy-done.11), kind=kOutput, calls=%fused_computation.40 | convolution fusion | flops 9970751 | bytes 823296 | tf_op jit(solution)/shard_map/bhlm,bmhd->blhd/dot_general | solution.py:352
  246.1 1.9 reshape.196
  247.9 2.0 concatenate.20
  250.0 2.0 fusion.5
  (74 shorter events, 50.1 us)
Async XLA Ops:
  0.6 6.0 %copy-start = (bf16[576,1152]{1,0:T(8,128)(2,1)S(1)}, bf16[576,1152]{1,0:T(8,128)(2,1)}, u32[]{:S(2)}) copy-start(bf16[576,1152]{1,0:T(8,128)(2,1)} %param.8) | copy-start | bytes 3981316
  2.2 1.8 copy-start.9
  2.5 1.5 copy-start.8
  3.7 0.6 copy-start.10
  4.3 0.7 copy-start.5
  5.5 1.1 copy-start.4
  5.5 3.3 %copy-start.1 = (bf16[2,64,1152]{2,1,0:T(8,128)(2,1)S(1)}, bf16[2,64,1152]{2,1,0:T(8,128)(2,1)}, u32[]{:S(2)}) copy-start(bf16[2,64,1152]{2,1,0:T(8,128)(2,1)} %param.11) | copy-start | bytes 884740
  5.5 3.3 %copy-start.2 = (bf16[576,1152]{1,0:T(8,128)(2,1)S(1)}, bf16[576,1152]{1,0:T(8,128)(2,1)}, u32[]{:S(2)}) copy-start(bf16[576,1152]{1,0:T(8,128)(2,1)} %param.10) | copy-start | bytes 3981316
  109.5 0.7 copy-start.6
  115.5 0.7 copy-start.7
  157.0 9.4 %copy-start.3 = (bf16[8,16,1152]{2,1,0:T(8,128)(2,1)S(1)}, bf16[8,16,1152]{2,1,0:T(8,128)(2,1)}, u32[]{:S(2)}) copy-start(bf16[8,16,1152]{2,1,0:T(8,128)(2,1)} %get-tuple-element.12) | copy-start | bytes 884740
  222.3 4.8 %copy-start.11 = (f32[2,8,64]{2,1,0:T(8,128)S(1)}, f32[2,8,64]{2,1,0:T(8,128)}, u32[]{:S(2)}) copy-start(f32[2,8,64]{2,1,0:T(8,128)} %copy-done.10) | copy-start | bytes 12292

commit v2 on v0

v2 whole, which is shorter than its diff:
```python
import functools
import math

import jax
import jax.numpy as jnp
import numpy as np
from jax import lax
from jax.experimental import pallas as pl
from jax.experimental.pallas import tpu as pltpu
from jax.sharding import PartitionSpec as P

DH = 72
HEADS = 8
HD = 576
D = 1152
ROWS = 128
COLS = 108
SCALE = 1.0 / math.sqrt(DH)
MESH = pl.DeviceIdType.MESH
BF = jnp.bfloat16
F32 = jnp.float32


def device(y, zh, zl, x, core):
    return (y * 4 + zh, (zl * 4 + x) * 2 + core)


def nt(left, right):
    return lax.dot_general(left, right, (((1,), (1,)), ((), ())), preferred_element_type=F32)


def tn(left, right):
    return lax.dot_general(left, right, (((0,), (0,)), ((), ())), preferred_element_type=F32)


def nn(left, right):
    return jnp.dot(left, right, preferred_element_type=F32)


def head(ref, n):
    return ref[:, n * DH : (n + 1) * DH]


def attend(qkv_ref, mask, p_ref, out_ref, heads):
    for h in heads:
        scores = nt(head(qkv_ref, h), head(qkv_ref, HEADS + h)) * SCALE
        scores = jnp.where(mask, scores, -1e30)
        scores = jnp.exp(scores - jnp.max(scores, axis=-1, keepdims=True))
        weights = scores / jnp.sum(scores, axis=-1, keepdims=True)
        p_ref[h] = weights
        out = nn(weights.astype(BF), head(qkv_ref, 2 * HEADS + h))
        out_ref[:, h * DH : (h + 1) * DH] = out.astype(BF)


def attend_grad(qkv_ref, p_ref, g_ref, grad_ref, heads):
    for h in heads:
        weights = p_ref[h]
        grad = head(g_ref, h)
        value_grad = tn(weights.astype(BF), grad)
        weight_grad = nt(grad, head(qkv_ref, 2 * HEADS + h))
        centered = weight_grad - jnp.sum(weights * weight_grad, axis=-1, keepdims=True)
        score_grad = (weights * centered * SCALE).astype(BF)
        query_grad = nn(score_grad, head(qkv_ref, HEADS + h))
        key_grad = tn(score_grad, head(qkv_ref, h))
        for part, value in enumerate((query_grad, key_grad, value_grad)):
            at = (part * HEADS + h) * DH
            grad_ref[:, at : at + DH] = value.astype(BF)


def to_peers(value, send_ref):
    for j in range(8):
        block = jnp.concatenate([value[8 * j : 8 * j + 8], value[64 + 8 * j : 72 + 8 * j]], axis=0)
        send_ref[j] = block.astype(BF)


def from_peers(recv_ref):
    blocks = [recv_ref[j].astype(F32) for j in range(8)]
    return jnp.concatenate([b[:8] for b in blocks] + [b[8:] for b in blocks], axis=0)


def kernel(
    tokens_hbm, sqkv_hbm, wos_hbm, w_hbm, wot_hbm, cot_hbm, pick_hbm,
    block_hbm, tgrad_hbm, sgrad_hbm, sums_hbm,
    tok, sqkv, wos, wraw, wpad, wot, cot, pick, wbuf,
    hid, hid_s, hid_r, og_s, og_r, pg_s, pg_r, to_s, to_r,
    ps_ref, pt_ref, so, tqkv, tqkvp, to, og, dqkv, tgrad, sog, sgrad, block, trow,
    lt, ltx, rx, gsend, grecv, ysend, yrecv, zsend, zrecv, sums,
    load_sems, out_sems, own_sem,
    zss, zrs, fss, frs, sss, srs, css, crs, ass, ars, oss, ors, xss, xrs, yss, yrs, rss, rrs,
):
    dp, seq = lax.axis_index("dp"), lax.axis_index("seq")
    y, zh, zl, x, c = dp // 4, dp % 4, seq // 8, (seq // 2) % 4, seq % 2
    u = (1 - c) * y + c * x
    v = (1 - c) * x + c * y
    zpos = zh * 4 + zl

    def at(u_, v_):
        return device((1 - c) * u_ + c * v_, zh, zl, (1 - c) * v_ + c * u_, c)

    partner = device(y, zh, zl, x, 1 - c)
    me = x * 2 + c
    peers = [(me + d) % 8 for d in range(1, 8)]
    peer_ids = [device(y, zh, zl, j // 2, j % 2) for j in peers]
    y_ids = [device((y + d) % 4, zh, zl, x, c) for d in range(1, 4)]
    x_ids = [device(y, zh, zl, (x + d) % 4, c) for d in range(1, 4)]
    z_at = [(zpos + d) % 16 for d in range(1, 16)]
    z_ids = [device(y, z // 4, z % 4, x, c) for z in z_at]
    everyone = peer_ids + y_ids + z_ids

    barrier = pltpu.get_barrier_semaphore()
    for target in everyone:
        pl.semaphore_signal(barrier, inc=1, device_id=target, device_id_type=MESH)

    loads = {}
    for n, (name, src, dst) in enumerate(
        (
            ("w", w_hbm, wraw), ("sqkv", sqkv_hbm, sqkv), ("cot", cot_hbm, cot), ("wot", wot_hbm, wot),
            ("wos", wos_hbm, wos), ("tok", tokens_hbm, tok), ("pick", pick_hbm, pick),
        )
    ):
        loads[name] = pltpu.make_async_copy(src, dst, load_sems.at[n])
        loads[name].start()
    pending = []

    def send(src, dst, send_sem, recv_sem, target):
        copy = pltpu.make_async_remote_copy(
            src_ref=src, dst_ref=dst, send_sem=send_sem, recv_sem=recv_sem,
            device_id=target, device_id_type=MESH,
        )
        copy.start()
        pending.append(copy)
        return copy

    loads["w"].wait()
    wpad[...] = jnp.concatenate([wraw[...], jnp.zeros((D, 128 - COLS), BF)], axis=1)

    def ring(slot, low, high, pos, ids, ss, rs):
        state = {}

        def start():
            ref = slot(pos)
            state["up"] = send(ref, ref, ss.at[0], rs.at[0], ids[0])
            state["down"] = send(ref, ref, ss.at[1], rs.at[1], ids[2])

        def relay():
            state["up"].wait_recv()
            ref = low(slot((pos + 3) % 4))
            state["up2"] = send(ref, ref, ss.at[2], rs.at[2], ids[0])
            state["down"].wait_recv()
            ref = high(slot((pos + 1) % 4))
            state["down2"] = send(ref, ref, ss.at[3], rs.at[3], ids[2])

        def finish():
            state["up2"].wait_recv()
            state["down2"].wait_recv()

        return start, relay, finish

    def piece_low(ref):
        return ref.at[pl.ds(0, 80)]

    def piece_high(ref):
        return ref.at[pl.ds(80, 64)]

    zring_ids = [device(y, (zh + d) % 4, zl, x, c) for d in range(1, 4)]
    u_ids = [at((u + d) % 4, v) for d in range(1, 4)]
    v_ids = [at(u, (v + d) % 4) for d in range(1, 4)]
    zr = ring(lambda p: wbuf.at[p, c, v, u], piece_low, piece_high, zh, zring_ids, zss, zrs)
    order = (0, 1, 3, 2)
    zsets = [(zh + 4 - e) % 4 for e in order]
    fr = [
        ring(lambda p, s=s: wbuf.at[s, c, v, p], piece_low, piece_high, u, u_ids, fss.at[i], frs.at[i])
        for i, s in enumerate(zsets)
    ]
    sr = [
        ring(
            lambda p, s=s: wbuf.at[s, c, p], lambda r: r.at[pl.ds(0, 2)], lambda r: r.at[pl.ds(2, 2)],
            v, v_ids, sss.at[i], srs.at[i],
        )
        for i, s in enumerate(zsets)
    ]
    crosses = {}

    def cross(i, d):
        ref = wbuf.at[zsets[i], c, (v + d) % 4]
        crosses[i, d] = send(ref, ref, css.at[i, d], crs.at[i, d], partner)

    def stage_c(i):
        fr[i][2]()
        sr[i][0]()
        cross(i, 0)

    def stage_d(i):
        sr[i][1]()
        cross(i, 3)
        cross(i, 1)

    def stage_e(i):
        sr[i][2]()
        cross(i, 2)

    def stage_f(i):
        for d in range(4):
            crosses[i, d].wait_recv()

    def gather():
        own = pltpu.make_async_copy(wpad.at[pl.ds((c * 4 + x) * 144, 144)], wbuf.at[zh, c, v, u], own_sem)
        own.start()
        own.wait()
        zr[0]()
        fr[0][0]()
        yield
        fr[0][1]()
        yield
        zr[1]()
        fr[1][0]()
        fr[2][0]()
        stage_c(0)
        yield
        fr[1][1]()
        fr[2][1]()
        stage_d(0)
        yield
        zr[2]()
        fr[3][0]()
        stage_c(1)
        stage_c(2)
        stage_e(0)
        yield
        fr[3][1]()
        stage_d(1)
        stage_d(2)
        yield
        stage_f(0)
        yield
        stage_c(3)
        stage_e(1)
        stage_e(2)
        yield
        stage_f(1)
        yield
        stage_d(3)
        yield
        stage_f(2)
        yield
        stage_e(3)
        yield
        stage_f(3)
        yield

    def exchange(n, src, dst):
        copies = []
        for d in (1, 7, 2, 6, 3, 5, 4):
            copies.append(
                send(src.at[peers[d - 1]], dst.at[me], ass.at[n, d - 1], ars.at[n, d - 1], peer_ids[d - 1])
            )
        dst[me] = src[me]
        return copies

    def arrived(copies):
        for copy in copies:
            copy.wait_recv()

    def weight_sum(w, left_ref, right_ref):
        lt[w] = nt(pick[...], left_ref[...]).astype(BF).reshape(2, 320, ROWS)
        swap = (
            send(lt.at[w, 1 - c], ltx.at[w], oss.at[w, 0], ors.at[w, 0], partner),
            send(right_ref, rx.at[w], oss.at[w, 1], ors.at[w, 1], partner),
        )
        yield
        arrived(swap)
        for xk in range(4):
            rows = pl.ds(xk * 80, 80)
            total = nn(lt[w, c, rows], right_ref[...]) + nn(ltx[w, rows], rx[w])
            for yk in range(4):
                gsend[w, (1 - c) * xk + c * yk, (1 - c) * yk + c * xk, :, 0:288] = total[
                    :, yk * 288 : (yk + 1) * 288
                ].astype(BF)
        first_at = (1 - c) * x + c * y
        second_at = (1 - c) * y + c * x

        def step_id(first, d):
            dx = (1 - c) * d if first else c * d
            dy = d - dx
            return device((y + dy) % 4, zh, zl, (x + dx) % 4, c)

        copies = [
            send(
                gsend.at[w, (first_at + d) % 4], grecv.at[w, d - 1], xss.at[w, d - 1], xrs.at[w, d - 1],
                step_id(True, d),
            )
            for d in (1, 3, 2)
        ]
        yield
        arrived(copies)
        for k in range(4):
            total = gsend[w, first_at, k].astype(F32)
            for d in range(3):
                total += grecv[w, d, k].astype(F32)
            ysend[w, k] = total.astype(BF)
        copies = [
            send(
                ysend.at[w, (second_at + d) % 4], yrecv.at[w, d - 1], yss.at[w, d - 1], yrs.at[w, d - 1],
                step_id(False, d),
            )
            for d in (1, 3, 2)
        ]
        yield
        arrived(copies)
        total = ysend[w, second_at].astype(F32)
        for d in range(3):
            total += yrecv[w, d].astype(F32)
        for zh_ in range(4):
            for zl_ in range(4):
                zsend[w, zh_ * 4 + zl_, 0:18, 0:72] = total[
                    zl_ * 18 : (zl_ + 1) * 18, zh_ * 72 : (zh_ + 1) * 72
                ].astype(BF)
        copies = [
            send(
                zsend.at[w, z_at[d - 1]], zrecv.at[w, d - 1], rss.at[w, d - 1], rrs.at[w, d - 1], z_ids[d - 1]
            )
            for d in range(1, 16)
        ]
        yield
        arrived(copies)
        total = zsend[w, zpos].astype(F32)
        for d in range(15):
            total += zrecv[w, d].astype(F32)
        sums[w] = total
        yield

    row = lax.broadcasted_iota(jnp.int32, (ROWS, ROWS), 0)
    col = lax.broadcasted_iota(jnp.int32, (ROWS, ROWS), 1)
    same_frame = (row // 64) == (col // 64)
    same_patch = (row % 8) == (col % 8)

    loads["cot"].wait()
    loads["wot"].wait()
    to_peers(nt(cot[...], wot[...]), og_s)
    loads["sqkv"].wait()

    pl.semaphore_wait(barrier, len(everyone))
    steps = gather()
    next(steps)
    attend(sqkv, same_frame, ps_ref, so, range(0, 2))
    next(steps)
    attend(sqkv, same_frame, ps_ref, so, range(2, 5))
    next(steps)
    attend(sqkv, same_frame, ps_ref, so, range(5, 8))
    next(steps)
    loads["wos"].wait()
    loads["tok"].wait()
    loads["pick"].wait()
    hidden = tok[...].astype(F32) + nn(so[...], wos[...])
    hid[...] = hidden.astype(BF)
    to_peers(hidden, hid_s)
    hidden_copies = exchange(0, hid_s, hid_r)
    grad_copies = exchange(1, og_s, og_r)
    next(steps)
    next(steps)
    arrived(hidden_copies)

    def shard_of(s, y_):
        upper = wbuf[s, 0, :, y_].reshape(HD, 128)
        lower = wbuf[s, 1, y_].reshape(HD, 128)
        return jnp.concatenate([upper, lower], axis=0)

    def project(i):
        rows = hid_r[...].reshape(ROWS, D)
        for pair in range(2):
            both = jnp.concatenate([shard_of(zsets[i], 2 * pair), shard_of(zsets[i], 2 * pair + 1)], axis=1)
            out = nn(rows, both).astype(BF)
            for k in range(2):
                tqkvp[(2 * pair + k) * 4 + zsets[i]] = out[:, k * 128 : (k + 1) * 128]

    for i in range(4):
        next(steps)
        if i < 3:
            next(steps)
        project(i)
    for s in range(16):
        tqkv[:, s * COLS : (s + 1) * COLS] = tqkvp[s, :, 0:COLS]

    attend(tqkv, same_patch, pt_ref, to, range(8))
    to_s[...] = to[...].reshape(8, 16, HD)
    out_copies = exchange(2, to_s, to_r)
    arrived(grad_copies)
    og[...] = og_r[...].reshape(ROWS, HD)
    attend_grad(tqkv, pt_ref, og, dqkv, range(8))
    total = None
    for pair in range(8):
        grads, weights = [], []
        for k in range(2):
            s = 2 * pair + k
            grads += [dqkv[:, s * COLS : (s + 1) * COLS], jnp.zeros((ROWS, 128 - COLS), BF)]
            weights.append(shard_of(s % 4, s // 4))
        part = nt(jnp.concatenate(grads, axis=1), jnp.concatenate(weights, axis=1))
        total = part if total is None else total + part
    pg_s[...] = total.astype(BF).reshape(8, 16, D)
    projection_copies = exchange(3, pg_s, pg_r)

    arrived(out_copies)
    rows = from_peers(to_r).astype(BF)
    trow[...] = rows
    temporal_sum = weight_sum(1, trow, cot)
    next(temporal_sum)
    block[...] = (hid[...].astype(F32) + nn(rows, wot[...])).astype(BF)
    outs = [pltpu.make_async_copy(block, block_hbm, out_sems.at[0])]
    outs[0].start()
    next(temporal_sum)
    arrived(projection_copies)
    tgrad[...] = (cot[...].astype(F32) + from_peers(pg_r)).astype(BF)
    outs.append(pltpu.make_async_copy(tgrad, tgrad_hbm, out_sems.at[1]))
    outs[1].start()
    spatial_sum = weight_sum(0, so, tgrad)
    next(spatial_sum)
    sog[...] = nt(tgrad[...], wos[...]).astype(BF)
    next(spatial_sum)
    next(temporal_sum)
    attend_grad(sqkv, ps_ref, sog, sgrad, range(0, 4))
    next(temporal_sum)
    attend_grad(sqkv, ps_ref, sog, sgrad, range(4, 8))
    outs.append(pltpu.make_async_copy(sgrad, sgrad_hbm, out_sems.at[2]))
    outs[2].start()
    next(spatial_sum)
    next(spatial_sum)
    next(temporal_sum)
    next(spatial_sum)
    outs.append(pltpu.make_async_copy(sums, sums_hbm, out_sems.at[3]))
    outs[3].start()
    for copy in outs:
        copy.wait()
    for copy in pending:
        copy.wait_send()


def picker():
    pick = np.zeros((2, 4, 80, HD), np.float32)
    for zl in range(4):
        for x in range(4):
            for core in range(2):
                for i in range(18):
                    pick[core, x, zl * 18 + i, ((zl * 4 + x) * 2 + core) * 18 + i] = 1
    return jnp.asarray(pick.reshape(640, HD), BF)


def shards(tokens, spatial_qkv, wo_spatial, w_temporal, wo_temporal, cotangent):
    frames, patches, _ = tokens.shape
    sems = pltpu.SemaphoreType.DMA

    def vm(*shape, dtype=BF):
        return pltpu.VMEM(shape, dtype)

    scratch = [
        vm(ROWS, D), vm(ROWS, 3 * HD), vm(HD, D), vm(D, COLS), vm(D, 128), vm(HD, D), vm(ROWS, D),
        vm(640, HD), vm(4, 2, 4, 4, 144, 128),
        vm(ROWS, D), vm(8, 16, D), vm(8, 16, D), vm(8, 16, HD), vm(8, 16, HD),
        vm(8, 16, D), vm(8, 16, D), vm(8, 16, HD), vm(8, 16, HD),
        vm(8, ROWS, ROWS, dtype=F32), vm(8, ROWS, ROWS, dtype=F32),
        vm(ROWS, HD), vm(ROWS, 3 * HD), vm(16, ROWS, 128), vm(ROWS, HD), vm(ROWS, HD),
        vm(ROWS, 3 * HD), vm(ROWS, D), vm(ROWS, HD), vm(ROWS, 3 * HD), vm(ROWS, D), vm(ROWS, HD),
        vm(2, 2, 320, ROWS), vm(2, 320, ROWS), vm(2, ROWS, D),
        vm(2, 4, 4, 80, 384), vm(2, 3, 4, 80, 384), vm(2, 4, 80, 384), vm(2, 3, 80, 384),
        vm(2, 16, 32, 128), vm(2, 15, 32, 128), vm(2, 32, 128, dtype=F32),
        sems((7,)), sems((4,)), sems,
        sems((4,)), sems((4,)), sems((4, 4)), sems((4, 4)), sems((4, 4)), sems((4, 4)),
        sems((4, 4)), sems((4, 4)), sems((4, 7)), sems((4, 7)), sems((2, 2)), sems((2, 2)),
        sems((2, 3)), sems((2, 3)), sems((2, 3)), sems((2, 3)), sems((2, 15)), sems((2, 15)),
    ]
    anywhere = pl.BlockSpec(memory_space=pl.ANY)
    block_out, tokens_grad, qkv_grad, sums = pl.pallas_call(
        kernel,
        out_shape=[
            jax.ShapeDtypeStruct((ROWS, D), BF), jax.ShapeDtypeStruct((ROWS, D), BF),
            jax.ShapeDtypeStruct((ROWS, 3 * HD), BF), jax.ShapeDtypeStruct((2, 32, 128), F32),
        ],
        in_specs=[anywhere] * 7,
        out_specs=[anywhere] * 4,
        scratch_shapes=scratch,
        compiler_params=pltpu.CompilerParams(
            collective_id=0, has_side_effects=True, vmem_limit_bytes=62 * 1024 * 1024
        ),
        name="block",
    )(
        tokens.reshape(ROWS, D), spatial_qkv.reshape(ROWS, 3 * HD), wo_spatial, w_temporal,
        wo_temporal, cotangent.reshape(ROWS, D), picker(),
    )
    return (
        block_out.reshape(frames, patches, D),
        tokens_grad.reshape(frames, patches, D),
        qkv_grad.reshape(frames, patches, 3 * HD),
        sums[0, :18, :72],
        sums[1, :18, :72],
    )


def solution(mesh):
    rows = P(("dp", "seq"), None, None)
    return jax.shard_map(
        shards,
        mesh=mesh,
        in_specs=(rows, rows, P(), P(None, "dp"), P(), rows),
        out_specs=(rows, rows, rows, P("seq", "dp"), P("seq", "dp")),
        check_vma=False,
    )
```

time: 742 us -> 100 us (0.13); the launches traced: 731 us -> 100 us
  waiting for transfers between devices: 607 us -> 0 us
  Pallas kernels: 0 us -> 92.1 us
  local copies, waits for them, and re-layouts: 43.8 us -> 7.4 us
  matrix products: 33.1 us -> 0 us
  starting transfers between devices: 29.1 us -> 0 us
  between operations: 15.5 us -> 0.65 us
    unnamed x5 -> x0, waiting for transfers between devices: 464 us -> none
    all_gather x1 -> x0, waiting for transfers between devices: 121 us -> none  [forward_project(): lax.all_gather(weight_shard, 'dp', axis=1, tiled=True)]
    pallas_call x0 -> x1, Pallas kernels: none -> 92.1 us  [shards(): pl.pallas_call(kernel, out_shape=[jax.ShapeDtypeStruct((ROWS, D), BF), ja...]
    dot_general x18 -> x0, matrix products: 29.7 us -> none  [the longest x3 5.09 us: times_transposed(): lax.dot_general(left, right, (((1,), (1,)), ((), ())), preferred_element_...]
    all_to_all x4 -> x0, starting transfers between devices: 29 us -> none  [the longest x1 11 us: shards(): lax.all_to_all(out_grad, 'seq', split_axis=1, concat_axis=0, tiled=True)]
    all_to_all x4 -> x0, waiting for transfers between devices: 22.3 us -> none  [the longest x1 11.5 us: shards(): lax.all_to_all(frame_qkv, 'seq', split_axis=1, concat_axis=0, tiled=True)]
    reshape x15 -> x0, local copies, waits for them, and re-layouts: 12.8 us -> none  [the longest x6 4.88 us: head_view(): return matrix.reshape(batch_size, length, inner_width // DH, DH)]
  transfers between devices with their start and end apart: 7 -> 0, of which waited for: 5 -> 0; matrix products, arithmetic and copies ran while one was open for 7% -> 0% of each run, Pallas kernels for 0% -> 0%
where the time goes in v2:
time: 100 us
  Pallas kernels  92.1 us (92%)
  local copies, waits for them, and re-layouts  7.4 us (7%)
    pallas_call x1, Pallas kernels, shards(): pl.pallas_call(kernel, out_shape=[jax.ShapeDtypeStruct((ROWS, D), BF), ja...  92.1 us
    unnamed x6, local copies, waits for them, and re-layouts  6.01 us

profile of v2, /device:TPU:1, one launch (start us, length us, event | category | flops | bytes accessed | tf_op | source)
XLA Modules:
  0.0 100.2 jit_solution(8504671135510962571)
XLA Ops:
  0.6 1.8 %copy.12.w_hbm = bf16[1152,108]{1,0:T(8,128)(2,1)} copy(bf16[1152,108]{0,1:T(8,128)(2,1)} %param.10) | data formatting | bytes 497664 | tf_op args[3]
  2.5 92.1 %block.1 = (bf16[128,1152]{1,0:T(8,128)(2,1)}, bf16[128,1152]{1,0:T(8,128)(2,1)}, bf16[128,1728]{1,0:T(8,128)(2,1)}, f32[2,32,128]{2,1,0:T(8,128)}) custom-call(bf16[128,1152]{1,0:T(8,128)(2,1)} %bitcast.12, bf16[128,1728]{1,0:T(8,128)(2,1)} %bitcast.10, bf16[576,1152]{1,0:T(8,128)(2,1)} %wos_hbm.1, bf16[1152,108]{1,0:T(8,128)(2,1)} %copy.12.w_hbm, ...), custom_call_target="tpu_custom_call" | custom-call | tf_op jit(solution)/shard_map/block/pallas_call | solution.py:471
  94.6 0.0 copy-start
  94.6 1.4 %slice_bitcast_fusion = (f32[18,72]{1,0:T(8,128)}, f32[18,72]{1,0:T(8,128)}) fusion(f32[2,32,128]{2,1,0:T(8,128)} %get-tuple-element.12), kind=kLoop, calls=%fused_computation | loop fusion | bytes 20736 | tf_op jit(solution)/shard_map/squeeze | solution.py:493
  96.0 1.7 %copy.16 = bf16[2,64,1152]{2,1,0:T(8,128)(2,1)} copy(bf16[2,64,1152]{2,1,0:T(8,128)(2,1)} %bitcast.15) | data formatting | bytes 589824
  97.7 1.7 %copy.17 = bf16[2,64,1152]{2,1,0:T(8,128)(2,1)} copy(bf16[2,64,1152]{2,1,0:T(8,128)(2,1)} %bitcast.14) | data formatting | bytes 589824
  99.4 0.0 copy-done
  99.4 0.8 copy.18
Async XLA Ops:
  94.6 4.8 %copy-start = (bf16[128,1728]{1,0:T(8,128)(2,1)S(1)}, bf16[128,1728]{1,0:T(8,128)(2,1)}, u32[]{:S(2)}) copy-start(bf16[128,1728]{1,0:T(8,128)(2,1)} %get-tuple-element.11) | copy-start | bytes 1327108

commit v3 on v2

--- a/solution.py
+++ b/solution.py
@@ -132,7 +132,8 @@
         return copy
 
     loads["w"].wait()
-    wpad[...] = jnp.concatenate([wraw[...], jnp.zeros((D, 128 - COLS), BF)], axis=1)
+    turned = wraw[...].astype(F32).T.astype(BF)
+    wpad[...] = jnp.concatenate([turned, jnp.zeros((D, 128 - COLS), BF)], axis=1)
 
     def ring(slot, low, high, pos, ids, ss, rs):
         state = {}
@@ -156,20 +157,31 @@
 
         return start, relay, finish
 
-    def piece_low(ref):
-        return ref.at[pl.ds(0, 80)]
-
-    def piece_high(ref):
-        return ref.at[pl.ds(80, 64)]
+    def direct(slot, pos, ids, ss, rs):
+        state = {}
+
+        def start():
+            ref = slot(pos)
+            for d in (2, 1, 3):
+                state[d] = send(ref, ref, ss.at[d - 1], rs.at[d - 1], ids[d - 1])
+
+        def near():
+            state[1].wait_recv()
+            state[3].wait_recv()
+
+        def far():
+            state[2].wait_recv()
+
+        return start, near, far
 
     zring_ids = [device(y, (zh + d) % 4, zl, x, c) for d in range(1, 4)]
     u_ids = [at((u + d) % 4, v) for d in range(1, 4)]
     v_ids = [at(u, (v + d) % 4) for d in range(1, 4)]
-    zr = ring(lambda p: wbuf.at[p, c, v, u], piece_low, piece_high, zh, zring_ids, zss, zrs)
+    zr = direct(lambda p: wbuf.at[p, c, v, u], zh, zring_ids, zss, zrs)
     order = (0, 1, 3, 2)
     zsets = [(zh + 4 - e) % 4 for e in order]
     fr = [
-        ring(lambda p, s=s: wbuf.at[s, c, v, p], piece_low, piece_high, u, u_ids, fss.at[i], frs.at[i])
+        direct(lambda p, s=s: wbuf.at[s, c, v, p], u, u_ids, fss.at[i], frs.at[i])
         for i, s in enumerate(zsets)
     ]
     sr = [
@@ -177,8 +189,9 @@
             lambda p, s=s: wbuf.at[s, c, p], lambda r: r.at[pl.ds(0, 2)], lambda r: r.at[pl.ds(2, 2)],
             v, v_ids, sss.at[i], srs.at[i],
         )
-        for i, s in enumerate(zsets)
+        for i, s in enumerate(zsets[:3])
     ]
+    sr.append(direct(lambda p: wbuf.at[zsets[3], c, p], v, v_ids, sss.at[3], srs.at[3]))
     crosses = {}
 
     def cross(i, d):
@@ -186,6 +199,7 @@
         crosses[i, d] = send(ref, ref, css.at[i, d], crs.at[i, d], partner)
 
     def stage_c(i):
+        fr[i][1]()
         fr[i][2]()
         sr[i][0]()
         cross(i, 0)
@@ -210,41 +224,31 @@
         zr[0]()
         fr[0][0]()
         yield
-        fr[0][1]()
-        yield
+        stage_c(0)
+        yield
+        stage_d(0)
         zr[1]()
         fr[1][0]()
         fr[2][0]()
-        stage_c(0)
-        yield
-        fr[1][1]()
-        fr[2][1]()
-        stage_d(0)
-        yield
+        stage_e(0)
+        stage_c(1)
+        stage_c(2)
         zr[2]()
         fr[3][0]()
-        stage_c(1)
-        stage_c(2)
-        stage_e(0)
-        yield
-        fr[3][1]()
         stage_d(1)
         stage_d(2)
+        stage_c(3)
         yield
         stage_f(0)
         yield
-        stage_c(3)
         stage_e(1)
+        stage_f(1)
+        yield
         stage_e(2)
-        yield
-        stage_f(1)
+        stage_f(2)
         yield
         stage_d(3)
-        yield
-        stage_f(2)
-        yield
         stage_e(3)
-        yield
         stage_f(3)
         yield
 
@@ -339,25 +343,21 @@
     to_peers(nt(cot[...], wot[...]), og_s)
     loads["sqkv"].wait()
 
-    pl.semaphore_wait(barrier, len(everyone))
-    steps = gather()
-    next(steps)
-    attend(sqkv, same_frame, ps_ref, so, range(0, 2))
-    next(steps)
-    attend(sqkv, same_frame, ps_ref, so, range(2, 5))
-    next(steps)
-    attend(sqkv, same_frame, ps_ref, so, range(5, 8))
-    next(steps)
+    attend(sqkv, same_frame, ps_ref, so, range(8))
     loads["wos"].wait()
     loads["tok"].wait()
     loads["pick"].wait()
     hidden = tok[...].astype(F32) + nn(so[...], wos[...])
     hid[...] = hidden.astype(BF)
     to_peers(hidden, hid_s)
+
+    pl.semaphore_wait(barrier, len(everyone))
+    steps = gather()
+    next(steps)
     hidden_copies = exchange(0, hid_s, hid_r)
-    grad_copies = exchange(1, og_s, og_r)
     next(steps)
     next(steps)
+    grad_copies = exchange(1, og_s, og_r)
     arrived(hidden_copies)
 
     def shard_of(s, y_):
@@ -375,8 +375,6 @@
 
     for i in range(4):
         next(steps)
-        if i < 3:
-            next(steps)
         project(i)
     for s in range(16):
         tqkv[:, s * COLS : (s + 1) * COLS] = tqkvp[s, :, 0:COLS]
@@ -434,6 +432,30 @@
         copy.wait_send()
 
 
+def finish_kernel(
+    block_hbm, tgrad_hbm, sgrad_hbm, sums_hbm, o1, o2, o3, o4, o5, block, tgrad, sgrad, sums, s1, s2, in_sems, out_sems
+):
+    ins = [
+        pltpu.make_async_copy(src, dst, in_sems.at[n])
+        for n, (src, dst) in enumerate(
+            ((sums_hbm, sums), (block_hbm, block), (tgrad_hbm, tgrad), (sgrad_hbm, sgrad))
+        )
+    ]
+    for copy in ins:
+        copy.start()
+    ins[0].wait()
+    s1[...] = sums[0, 0:18, 0:72]
+    s2[...] = sums[1, 0:18, 0:72]
+    outs = []
+    for n, (src, dst) in enumerate(((s1, o4), (s2, o5), (block, o1), (tgrad, o2), (sgrad, o3))):
+        if n >= 2:
+            ins[n - 1].wait()
+        outs.append(pltpu.make_async_copy(src, dst, out_sems.at[n]))
+        outs[-1].start()
+    for copy in outs:
+        copy.wait()
+
+
 def picker():
     pick = np.zeros((2, 4, 80, HD), np.float32)
     for zl in range(4):
@@ -452,7 +474,7 @@
         return pltpu.VMEM(shape, dtype)
 
     scratch = [
-        vm(ROWS, D), vm(ROWS, 3 * HD), vm(HD, D), vm(D, COLS), vm(D, 128), vm(HD, D), vm(ROWS, D),
+        vm(ROWS, D), vm(ROWS, 3 * HD), vm(HD, D), vm(COLS, D), vm(D, 128), vm(HD, D), vm(ROWS, D),
         vm(640, HD), vm(4, 2, 4, 4, 144, 128),
         vm(ROWS, D), vm(8, 16, D), vm(8, 16, D), vm(8, 16, HD), vm(8, 16, HD),
         vm(8, 16, D), vm(8, 16, D), vm(8, 16, HD), vm(8, 16, HD),
@@ -482,15 +504,30 @@
         ),
         name="block",
     )(
-        tokens.reshape(ROWS, D), spatial_qkv.reshape(ROWS, 3 * HD), wo_spatial, w_temporal,
+        tokens.reshape(ROWS, D), spatial_qkv.reshape(ROWS, 3 * HD), wo_spatial, w_temporal.T,
         wo_temporal, cotangent.reshape(ROWS, D), picker(),
     )
+    block_out, tokens_grad, qkv_grad, spatial_sum, temporal_sum = pl.pallas_call(
+        finish_kernel,
+        out_shape=[
+            jax.ShapeDtypeStruct((ROWS, D), BF), jax.ShapeDtypeStruct((ROWS, D), BF),
+            jax.ShapeDtypeStruct((ROWS, 3 * HD), BF),
+            jax.ShapeDtypeStruct((18, 72), F32), jax.ShapeDtypeStruct((18, 72), F32),
+        ],
+        in_specs=[anywhere] * 4,
+        out_specs=[anywhere] * 5,
+        scratch_shapes=[
+            vm(ROWS, D), vm(ROWS, D), vm(ROWS, 3 * HD), vm(2, 32, 128, dtype=F32),
+            vm(18, 72, dtype=F32), vm(18, 72, dtype=F32), sems((4,)), sems((5,)),
+        ],
+        name="finish",
+    )(block_out, tokens_grad, qkv_grad, sums)
     return (
         block_out.reshape(frames, patches, D),
         tokens_grad.reshape(frames, patches, D),
         qkv_grad.reshape(frames, patches, 3 * HD),
-        sums[0, :18, :72],
-        sums[1, :18, :72],
+        spatial_sum,
+        temporal_sum,
     )
 
 

time: 100 us -> 93.1 us (0.931)
  local copies, waits for them, and re-layouts: 7.4 us -> 0 us
    unnamed x6 -> x0, local copies, waits for them, and re-layouts: 6.01 us -> none
    pallas_call x1, Pallas kernels: 92.1 us -> 89.6 us  [shards(): pl.pallas_call(kernel, out_shape=[jax.ShapeDtypeStruct((ROWS, D), BF), ja...]
    pallas_call x0 -> x1, Pallas kernels: none -> 2.06 us  [shards(): pl.pallas_call(finish_kernel, out_shape=[jax.ShapeDtypeStruct((ROWS, D),...]
    squeeze x1 -> x0, local copies, waits for them, and re-layouts: 1.38 us -> none  [shards(): sums[1, :18, :72]]
where the time goes in v3:
time: 93.1 us; the launch traced here: 92.5 us
  Pallas kernels  91.7 us (98%)
    pallas_call x1, Pallas kernels, shards(): pl.pallas_call(kernel, out_shape=[jax.ShapeDtypeStruct((ROWS, D), BF), ja...  89.6 us
    pallas_call x1, Pallas kernels, shards(): pl.pallas_call(finish_kernel, out_shape=[jax.ShapeDtypeStruct((ROWS, D),...  2.06 us

profile of v3, /device:TPU:1, one launch (start us, length us, event | category | flops | bytes accessed | tf_op | source)
XLA Modules:
  0.0 92.5 jit_solution(11981644113044228924)
XLA Ops:
  0.6 89.6 %block.1 = (bf16[128,1152]{1,0:T(8,128)(2,1)}, bf16[128,1152]{1,0:T(8,128)(2,1)}, bf16[128,1728]{1,0:T(8,128)(2,1)}, f32[2,32,128]{2,1,0:T(8,128)}) custom-call(bf16[128,1152]{1,0:T(8,128)(2,1)} %bitcast.8, bf16[128,1728]{1,0:T(8,128)(2,1)} %bitcast.7, bf16[576,1152]{1,0:T(8,128)(2,1)} %wos_hbm.1, bf16[108,1152]{1,0:T(8,128)(2,1)} %bitcast.10, ...), custom_call_target="tpu_custom_call" | custom-call | tf_op jit(solution)/shard_map/block/pallas_call | solution.py:493
  90.2 2.1 %finish.1 = (bf16[128,1152]{1,0:T(8,128)(2,1)}, bf16[128,1152]{1,0:T(8,128)(2,1)}, bf16[128,1728]{1,0:T(8,128)(2,1)}, f32[18,72]{1,0:T(8,128)}, f32[18,72]{1,0:T(8,128)}) custom-call(bf16[128,1152]{1,0:T(8,128)(2,1)} %get-tuple-element.14.block_hbm, bf16[128,1152]{1,0:T(8,128)(2,1)} %get-tuple-element.15.tgrad_hbm, ...), custom_call_target="tpu_custom_call" | custom-call | tf_op jit(solution)/shard_map/finish/pallas_call | solution.py:510

commit v4 on v3

--- a/solution.py
+++ b/solution.py
@@ -82,9 +82,9 @@
     tokens_hbm, sqkv_hbm, wos_hbm, w_hbm, wot_hbm, cot_hbm, pick_hbm,
     block_hbm, tgrad_hbm, sgrad_hbm, sums_hbm,
     tok, sqkv, wos, wraw, wpad, wot, cot, pick, wbuf,
-    hid, hid_s, hid_r, og_s, og_r, pg_s, pg_r, to_s, to_r,
-    ps_ref, pt_ref, so, tqkv, tqkvp, to, og, dqkv, tgrad, sog, sgrad, block, trow,
-    lt, ltx, rx, gsend, grecv, ysend, yrecv, zsend, zrecv, sums,
+    hid, hid_s, hid_r, cot_s, cot_r, tg_s, tg_r, to_s, to_r,
+    ps_ref, pt_ref, so, tqkv, tqkvp, to, og, dqkv, tgrad, sog, sgrad, block,
+    so_s, so_r, cotx, tgx, lt, ltx, gsend, grecv, ysend, yrecv, zsend, zrecv, sums,
     load_sems, out_sems, own_sem,
     zss, zrs, fss, frs, sss, srs, css, crs, ass, ars, oss, ors, xss, xrs, yss, yrs, rss, rrs,
 ):
@@ -134,6 +134,8 @@
     loads["w"].wait()
     turned = wraw[...].astype(F32).T.astype(BF)
     wpad[...] = jnp.concatenate([turned, jnp.zeros((D, 128 - COLS), BF)], axis=1)
+    own = pltpu.make_async_copy(wpad.at[pl.ds((c * 4 + x) * 144, 144)], wbuf.at[zh, c, v, u], own_sem)
+    own.start()
 
     def ring(slot, low, high, pos, ids, ss, rs):
         state = {}
@@ -189,9 +191,9 @@
             lambda p, s=s: wbuf.at[s, c, p], lambda r: r.at[pl.ds(0, 2)], lambda r: r.at[pl.ds(2, 2)],
             v, v_ids, sss.at[i], srs.at[i],
         )
-        for i, s in enumerate(zsets[:3])
+        for i, s in enumerate(zsets)
     ]
-    sr.append(direct(lambda p: wbuf.at[zsets[3], c, p], v, v_ids, sss.at[3], srs.at[3]))
+
     crosses = {}
 
     def cross(i, d):
@@ -218,36 +220,32 @@
             crosses[i, d].wait_recv()
 
     def gather():
-        own = pltpu.make_async_copy(wpad.at[pl.ds((c * 4 + x) * 144, 144)], wbuf.at[zh, c, v, u], own_sem)
-        own.start()
-        own.wait()
         zr[0]()
         fr[0][0]()
-        yield
         stage_c(0)
-        yield
-        stage_d(0)
         zr[1]()
         fr[1][0]()
         fr[2][0]()
-        stage_e(0)
+        stage_d(0)
+        zr[2]()
+        fr[3][0]()
         stage_c(1)
         stage_c(2)
-        zr[2]()
-        fr[3][0]()
+        yield
+        stage_e(0)
+        stage_c(3)
         stage_d(1)
         stage_d(2)
-        stage_c(3)
+        stage_d(3)
         yield
         stage_f(0)
         yield
         stage_e(1)
+        stage_e(2)
         stage_f(1)
         yield
-        stage_e(2)
         stage_f(2)
         yield
-        stage_d(3)
         stage_e(3)
         stage_f(3)
         yield
@@ -265,21 +263,31 @@
         for copy in copies:
             copy.wait_recv()
 
-    def weight_sum(w, left_ref, right_ref):
-        lt[w] = nt(pick[...], left_ref[...]).astype(BF).reshape(2, 320, ROWS)
-        swap = (
-            send(lt.at[w, 1 - c], ltx.at[w], oss.at[w, 0], ors.at[w, 0], partner),
-            send(right_ref, rx.at[w], oss.at[w, 1], ors.at[w, 1], partner),
-        )
-        yield
-        arrived(swap)
+    def left_operand(n, value):
+        lt[n] = nt(pick[...], value).astype(BF).reshape(2, 320, ROWS)
+        return send(lt.at[n, 1 - c], ltx.at[n], oss.at[n], ors.at[n], partner)
+
+    def weight_sum(w, product):
         for xk in range(4):
-            rows = pl.ds(xk * 80, 80)
-            total = nn(lt[w, c, rows], right_ref[...]) + nn(ltx[w, rows], rx[w])
+            total = product(pl.ds(xk * 80, 80), xk)
             for yk in range(4):
-                gsend[w, (1 - c) * xk + c * yk, (1 - c) * yk + c * xk, :, 0:288] = total[
-                    :, yk * 288 : (yk + 1) * 288
-                ].astype(BF)
+                first, second = (1 - c) * xk + c * yk, (1 - c) * yk + c * xk
+                for k in range(2):
+                    at_ = yk * 288 + k * 128
+                    gsend[w, first, 2 * second + k] = total[:, at_ : at_ + 128].astype(BF)
+            rests = [total[:, yk * 288 + 256 : yk * 288 + 288].astype(BF) for yk in range(4)]
+
+            @pl.when(c == 0)
+            def _():
+                for yk in range(4):
+                    gsend[w, xk, 8, :, yk * 32 : yk * 32 + 32] = rests[yk]
+
+            @pl.when(c == 1)
+            def _():
+                for yk in range(4):
+                    gsend[w, yk, 8, :, xk * 32 : xk * 32 + 32] = rests[yk]
+
+        yield
         first_at = (1 - c) * x + c * y
         second_at = (1 - c) * y + c * x
 
@@ -297,11 +305,18 @@
         ]
         yield
         arrived(copies)
-        for k in range(4):
+
+        def first_sum(k):
             total = gsend[w, first_at, k].astype(F32)
             for d in range(3):
                 total += grecv[w, d, k].astype(F32)
-            ysend[w, k] = total.astype(BF)
+            return total.astype(BF)
+
+        rest = first_sum(8)
+        for k in range(4):
+            ysend[w, k, :, 0:128] = first_sum(2 * k)
+            ysend[w, k, :, 128:256] = first_sum(2 * k + 1)
+            ysend[w, k, :, 256:288] = rest[:, k * 32 : k * 32 + 32]
         copies = [
             send(
                 ysend.at[w, (second_at + d) % 4], yrecv.at[w, d - 1], yss.at[w, d - 1], yrs.at[w, d - 1],
@@ -323,7 +338,7 @@
             send(
                 zsend.at[w, z_at[d - 1]], zrecv.at[w, d - 1], rss.at[w, d - 1], rrs.at[w, d - 1], z_ids[d - 1]
             )
-            for d in range(1, 16)
+            for d in (8, 7, 9, 6, 10, 5, 11, 4, 12, 3, 13, 2, 14, 1, 15)
         ]
         yield
         arrived(copies)
@@ -339,25 +354,27 @@
     same_patch = (row % 8) == (col % 8)
 
     loads["cot"].wait()
-    loads["wot"].wait()
-    to_peers(nt(cot[...], wot[...]), og_s)
+    to_peers(cot[...].astype(F32), cot_s)
     loads["sqkv"].wait()
 
     attend(sqkv, same_frame, ps_ref, so, range(8))
     loads["wos"].wait()
     loads["tok"].wait()
     loads["pick"].wait()
+    loads["wot"].wait()
     hidden = tok[...].astype(F32) + nn(so[...], wos[...])
     hid[...] = hidden.astype(BF)
+    to_peers(so[...].astype(F32), so_s)
     to_peers(hidden, hid_s)
 
+    own.wait()
     pl.semaphore_wait(barrier, len(everyone))
     steps = gather()
     next(steps)
     hidden_copies = exchange(0, hid_s, hid_r)
     next(steps)
-    next(steps)
-    grad_copies = exchange(1, og_s, og_r)
+    cot_copies = exchange(1, cot_s, cot_r)
+    spatial_copies = exchange(4, so_s, so_r)
     arrived(hidden_copies)
 
     def shard_of(s, y_):
@@ -379,12 +396,30 @@
     for s in range(16):
         tqkv[:, s * COLS : (s + 1) * COLS] = tqkvp[s, :, 0:COLS]
 
+    arrived(cot_copies)
+    cot_swap = send(cot_r, cotx, oss.at[2], ors.at[2], partner)
     attend(tqkv, same_patch, pt_ref, to, range(8))
     to_s[...] = to[...].reshape(8, 16, HD)
     out_copies = exchange(2, to_s, to_r)
-    arrived(grad_copies)
-    og[...] = og_r[...].reshape(ROWS, HD)
+    temporal_left = left_operand(1, to[...])
+    og[...] = nt(cot_r[...].reshape(ROWS, D), wot[...]).astype(BF)
+    arrived(spatial_copies)
+    spatial_left = left_operand(0, so_r[...].reshape(ROWS, HD))
     attend_grad(tqkv, pt_ref, og, dqkv, range(8))
+
+    def temporal_product(part, xk):
+        mine = nn(lt[1, c, part], cot_r[...].reshape(ROWS, D))
+        return mine + nn(ltx[1, part], cotx[...].reshape(ROWS, D))
+
+    def spatial_product(part, xk):
+        mine = nn(lt[0, c, part], tg_s[...].reshape(ROWS, D))
+        return mine + nn(ltx[0, part], tgx[...].reshape(ROWS, D))
+
+    temporal_sum = weight_sum(1, temporal_product)
+    spatial_sum = weight_sum(0, spatial_product)
+    arrived((temporal_left, cot_swap))
+    next(temporal_sum)
+    next(temporal_sum)
     total = None
     for pair in range(8):
         grads, weights = [], []
@@ -394,34 +429,31 @@
             weights.append(shard_of(s % 4, s // 4))
         part = nt(jnp.concatenate(grads, axis=1), jnp.concatenate(weights, axis=1))
         total = part if total is None else total + part
-    pg_s[...] = total.astype(BF).reshape(8, 16, D)
-    projection_copies = exchange(3, pg_s, pg_r)
+    total = cot_r[...].reshape(ROWS, D).astype(F32) + total.astype(BF).astype(F32)
+    tg_s[...] = total.astype(BF).reshape(8, 16, D)
+    tg_swap = send(tg_s, tgx, oss.at[3], ors.at[3], partner)
+    tokens_copies = exchange(3, tg_s, tg_r)
+    arrived((tg_swap, spatial_left))
+    next(spatial_sum)
+    next(spatial_sum)
 
     arrived(out_copies)
-    rows = from_peers(to_r).astype(BF)
-    trow[...] = rows
-    temporal_sum = weight_sum(1, trow, cot)
-    next(temporal_sum)
-    block[...] = (hid[...].astype(F32) + nn(rows, wot[...])).astype(BF)
+    block[...] = (hid[...].astype(F32) + nn(from_peers(to_r).astype(BF), wot[...])).astype(BF)
     outs = [pltpu.make_async_copy(block, block_hbm, out_sems.at[0])]
     outs[0].start()
     next(temporal_sum)
-    arrived(projection_copies)
-    tgrad[...] = (cot[...].astype(F32) + from_peers(pg_r)).astype(BF)
+    arrived(tokens_copies)
+    tgrad[...] = from_peers(tg_r).astype(BF)
     outs.append(pltpu.make_async_copy(tgrad, tgrad_hbm, out_sems.at[1]))
     outs[1].start()
-    spatial_sum = weight_sum(0, so, tgrad)
+    sog[...] = nt(tgrad[...], wos[...]).astype(BF)
+    next(temporal_sum)
     next(spatial_sum)
-    sog[...] = nt(tgrad[...], wos[...]).astype(BF)
+    attend_grad(sqkv, ps_ref, sog, sgrad, range(0, 4))
     next(spatial_sum)
-    next(temporal_sum)
-    attend_grad(sqkv, ps_ref, sog, sgrad, range(0, 4))
-    next(temporal_sum)
     attend_grad(sqkv, ps_ref, sog, sgrad, range(4, 8))
     outs.append(pltpu.make_async_copy(sgrad, sgrad_hbm, out_sems.at[2]))
     outs[2].start()
-    next(spatial_sum)
-    next(spatial_sum)
     next(temporal_sum)
     next(spatial_sum)
     outs.append(pltpu.make_async_copy(sums, sums_hbm, out_sems.at[3]))
@@ -476,17 +508,18 @@
     scratch = [
         vm(ROWS, D), vm(ROWS, 3 * HD), vm(HD, D), vm(COLS, D), vm(D, 128), vm(HD, D), vm(ROWS, D),
         vm(640, HD), vm(4, 2, 4, 4, 144, 128),
-        vm(ROWS, D), vm(8, 16, D), vm(8, 16, D), vm(8, 16, HD), vm(8, 16, HD),
+        vm(ROWS, D), vm(8, 16, D), vm(8, 16, D), vm(8, 16, D), vm(8, 16, D),
         vm(8, 16, D), vm(8, 16, D), vm(8, 16, HD), vm(8, 16, HD),
         vm(8, ROWS, ROWS, dtype=F32), vm(8, ROWS, ROWS, dtype=F32),
         vm(ROWS, HD), vm(ROWS, 3 * HD), vm(16, ROWS, 128), vm(ROWS, HD), vm(ROWS, HD),
-        vm(ROWS, 3 * HD), vm(ROWS, D), vm(ROWS, HD), vm(ROWS, 3 * HD), vm(ROWS, D), vm(ROWS, HD),
-        vm(2, 2, 320, ROWS), vm(2, 320, ROWS), vm(2, ROWS, D),
-        vm(2, 4, 4, 80, 384), vm(2, 3, 4, 80, 384), vm(2, 4, 80, 384), vm(2, 3, 80, 384),
+        vm(ROWS, 3 * HD), vm(ROWS, D), vm(ROWS, HD), vm(ROWS, 3 * HD), vm(ROWS, D),
+        vm(8, 16, HD), vm(8, 16, HD), vm(8, 16, D), vm(8, 16, D),
+        vm(2, 2, 320, ROWS), vm(2, 320, ROWS),
+        vm(2, 4, 9, 80, 128), vm(2, 3, 9, 80, 128), vm(2, 4, 80, 384), vm(2, 3, 80, 384),
         vm(2, 16, 32, 128), vm(2, 15, 32, 128), vm(2, 32, 128, dtype=F32),
         sems((7,)), sems((4,)), sems,
         sems((4,)), sems((4,)), sems((4, 4)), sems((4, 4)), sems((4, 4)), sems((4, 4)),
-        sems((4, 4)), sems((4, 4)), sems((4, 7)), sems((4, 7)), sems((2, 2)), sems((2, 2)),
+        sems((4, 4)), sems((4, 4)), sems((5, 7)), sems((5, 7)), sems((4,)), sems((4,)),
         sems((2, 3)), sems((2, 3)), sems((2, 3)), sems((2, 3)), sems((2, 15)), sems((2, 15)),
     ]
     anywhere = pl.BlockSpec(memory_space=pl.ANY)

time: 93.1 us -> 89.7 us (0.963)
  the two profiles are of different devices: /device:TPU:1 before, /device:TPU:2 now
where the time goes in v4:
time: 89.7 us; the launch traced here: 89.6 us
  Pallas kernels  88.8 us (99%)
    pallas_call x1, Pallas kernels, shards(): pl.pallas_call(kernel, out_shape=[jax.ShapeDtypeStruct((ROWS, D), BF), ja...  86.7 us
    pallas_call x1, Pallas kernels, shards(): pl.pallas_call(finish_kernel, out_shape=[jax.ShapeDtypeStruct((ROWS, D),...  2.06 us

profile of v4, /device:TPU:2, one launch (start us, length us, event | category | flops | bytes accessed | tf_op | source)
XLA Modules:
  0.0 89.6 jit_solution(8459966693791769573)
XLA Ops:
  0.6 86.7 %block.1 = (bf16[128,1152]{1,0:T(8,128)(2,1)}, bf16[128,1152]{1,0:T(8,128)(2,1)}, bf16[128,1728]{1,0:T(8,128)(2,1)}, f32[2,32,128]{2,1,0:T(8,128)}) custom-call(bf16[128,1152]{1,0:T(8,128)(2,1)} %bitcast.8, bf16[128,1728]{1,0:T(8,128)(2,1)} %bitcast.7, bf16[576,1152]{1,0:T(8,128)(2,1)} %wos_hbm.1, bf16[108,1152]{1,0:T(8,128)(2,1)} %bitcast.10, ...), custom_call_target="tpu_custom_call" | custom-call | tf_op jit(solution)/shard_map/block/pallas_call | solution.py:526
  87.4 2.1 %finish.1 = (bf16[128,1152]{1,0:T(8,128)(2,1)}, bf16[128,1152]{1,0:T(8,128)(2,1)}, bf16[128,1728]{1,0:T(8,128)(2,1)}, f32[18,72]{1,0:T(8,128)}, f32[18,72]{1,0:T(8,128)}) custom-call(bf16[128,1152]{1,0:T(8,128)(2,1)} %get-tuple-element.14.block_hbm, bf16[128,1152]{1,0:T(8,128)(2,1)} %get-tuple-element.15.tgrad_hbm, ...), custom_call_target="tpu_custom_call" | custom-call | tf_op jit(solution)/shard_map/finish/pallas_call | solution.py:543

commit v5 on v4

--- a/solution.py
+++ b/solution.py
@@ -252,7 +252,7 @@
 
     def exchange(n, src, dst):
         copies = []
-        for d in (1, 7, 2, 6, 3, 5, 4):
+        for d in (4, 3, 5, 2, 6, 1, 7):
             copies.append(
                 send(src.at[peers[d - 1]], dst.at[me], ass.at[n, d - 1], ars.at[n, d - 1], peer_ids[d - 1])
             )
@@ -301,7 +301,7 @@
                 gsend.at[w, (first_at + d) % 4], grecv.at[w, d - 1], xss.at[w, d - 1], xrs.at[w, d - 1],
                 step_id(True, d),
             )
-            for d in (1, 3, 2)
+            for d in (2, 1, 3)
         ]
         yield
         arrived(copies)
@@ -322,7 +322,7 @@
                 ysend.at[w, (second_at + d) % 4], yrecv.at[w, d - 1], yss.at[w, d - 1], yrs.at[w, d - 1],
                 step_id(False, d),
             )
-            for d in (1, 3, 2)
+            for d in (2, 1, 3)
         ]
         yield
         arrived(copies)
@@ -331,9 +331,10 @@
             total += yrecv[w, d].astype(F32)
         for zh_ in range(4):
             for zl_ in range(4):
-                zsend[w, zh_ * 4 + zl_, 0:18, 0:72] = total[
-                    zl_ * 18 : (zl_ + 1) * 18, zh_ * 72 : (zh_ + 1) * 72
-                ].astype(BF)
+                chunk = total[zl_ * 18 : (zl_ + 1) * 18, zh_ * 72 : (zh_ + 1) * 72].astype(BF)
+                zsend[w, zh_ * 4 + zl_, :, 0:72] = chunk[0:16]
+                zsend[w, zh_ * 4 + zl_, 0:2, 72:108] = chunk[16:18, 0:36]
+                zsend[w, zh_ * 4 + zl_, 2:4, 72:108] = chunk[16:18, 36:72]
         copies = [
             send(
                 zsend.at[w, z_at[d - 1]], zrecv.at[w, d - 1], rss.at[w, d - 1], rrs.at[w, d - 1], z_ids[d - 1]
@@ -369,9 +370,9 @@
 
     own.wait()
     pl.semaphore_wait(barrier, len(everyone))
+    hidden_copies = exchange(0, hid_s, hid_r)
     steps = gather()
     next(steps)
-    hidden_copies = exchange(0, hid_s, hid_r)
     next(steps)
     cot_copies = exchange(1, cot_s, cot_r)
     spatial_copies = exchange(4, so_s, so_r)
@@ -405,8 +406,6 @@
     og[...] = nt(cot_r[...].reshape(ROWS, D), wot[...]).astype(BF)
     arrived(spatial_copies)
     spatial_left = left_operand(0, so_r[...].reshape(ROWS, HD))
-    attend_grad(tqkv, pt_ref, og, dqkv, range(8))
-
     def temporal_product(part, xk):
         mine = nn(lt[1, c, part], cot_r[...].reshape(ROWS, D))
         return mine + nn(ltx[1, part], cotx[...].reshape(ROWS, D))
@@ -420,6 +419,8 @@
     arrived((temporal_left, cot_swap))
     next(temporal_sum)
     next(temporal_sum)
+    attend_grad(tqkv, pt_ref, og, dqkv, range(8))
+
     total = None
     for pair in range(8):
         grads, weights = [], []
@@ -433,6 +434,7 @@
     tg_s[...] = total.astype(BF).reshape(8, 16, D)
     tg_swap = send(tg_s, tgx, oss.at[3], ors.at[3], partner)
     tokens_copies = exchange(3, tg_s, tg_r)
+    next(temporal_sum)
     arrived((tg_swap, spatial_left))
     next(spatial_sum)
     next(spatial_sum)
@@ -447,7 +449,6 @@
     outs.append(pltpu.make_async_copy(tgrad, tgrad_hbm, out_sems.at[1]))
     outs[1].start()
     sog[...] = nt(tgrad[...], wos[...]).astype(BF)
-    next(temporal_sum)
     next(spatial_sum)
     attend_grad(sqkv, ps_ref, sog, sgrad, range(0, 4))
     next(spatial_sum)
@@ -476,8 +477,10 @@
     for copy in ins:
         copy.start()
     ins[0].wait()
-    s1[...] = sums[0, 0:18, 0:72]
-    s2[...] = sums[1, 0:18, 0:72]
+    for n, out in enumerate((s1, s2)):
+        out[0:16] = sums[n, :, 0:72]
+        out[16:18, 0:36] = sums[n, 0:2, 72:108]
+        out[16:18, 36:72] = sums[n, 2:4, 72:108]
     outs = []
     for n, (src, dst) in enumerate(((s1, o4), (s2, o5), (block, o1), (tgrad, o2), (sgrad, o3))):
         if n >= 2:
@@ -516,7 +519,7 @@
         vm(8, 16, HD), vm(8, 16, HD), vm(8, 16, D), vm(8, 16, D),
         vm(2, 2, 320, ROWS), vm(2, 320, ROWS),
         vm(2, 4, 9, 80, 128), vm(2, 3, 9, 80, 128), vm(2, 4, 80, 384), vm(2, 3, 80, 384),
-        vm(2, 16, 32, 128), vm(2, 15, 32, 128), vm(2, 32, 128, dtype=F32),
+        vm(2, 16, 16, 128), vm(2, 15, 16, 128), vm(2, 16, 128, dtype=F32),
         sems((7,)), sems((4,)), sems,
         sems((4,)), sems((4,)), sems((4, 4)), sems((4, 4)), sems((4, 4)), sems((4, 4)),
         sems((4, 4)), sems((4, 4)), sems((5, 7)), sems((5, 7)), sems((4,)), sems((4,)),
@@ -527,7 +530,7 @@
         kernel,
         out_shape=[
             jax.ShapeDtypeStruct((ROWS, D), BF), jax.ShapeDtypeStruct((ROWS, D), BF),
-            jax.ShapeDtypeStruct((ROWS, 3 * HD), BF), jax.ShapeDtypeStruct((2, 32, 128), F32),
+            jax.ShapeDtypeStruct((ROWS, 3 * HD), BF), jax.ShapeDtypeStruct((2, 16, 128), F32),
         ],
         in_specs=[anywhere] * 7,
         out_specs=[anywhere] * 4,
@@ -550,7 +553,7 @@
         in_specs=[anywhere] * 4,
         out_specs=[anywhere] * 5,
         scratch_shapes=[
-            vm(ROWS, D), vm(ROWS, D), vm(ROWS, 3 * HD), vm(2, 32, 128, dtype=F32),
+            vm(ROWS, D), vm(ROWS, D), vm(ROWS, 3 * HD), vm(2, 16, 128, dtype=F32),
             vm(18, 72, dtype=F32), vm(18, 72, dtype=F32), sems((4,)), sems((5,)),
         ],
         name="finish",

time: 89.7 us -> 83.6 us (0.932)
  the two profiles are of different devices: /device:TPU:2 before, /device:TPU:1 now
where the time goes in v5:
time: 83.6 us; the launch traced here: 83.4 us
  Pallas kernels  82.6 us (99%)
    pallas_call x1, Pallas kernels, shards(): pl.pallas_call(kernel, out_shape=[jax.ShapeDtypeStruct((ROWS, D), BF), ja...  80.6 us
    pallas_call x1, Pallas kernels, shards(): pl.pallas_call(finish_kernel, out_shape=[jax.ShapeDtypeStruct((ROWS, D),...  2.06 us

profile of v5, /device:TPU:1, one launch (start us, length us, event | category | flops | bytes accessed | tf_op | source)
XLA Modules:
  0.0 83.4 jit_solution(7381555447296561889)
XLA Ops:
  0.6 80.6 %block.1 = (bf16[128,1152]{1,0:T(8,128)(2,1)}, bf16[128,1152]{1,0:T(8,128)(2,1)}, bf16[128,1728]{1,0:T(8,128)(2,1)}, f32[2,16,128]{2,1,0:T(8,128)}) custom-call(bf16[128,1152]{1,0:T(8,128)(2,1)} %bitcast.8, bf16[128,1728]{1,0:T(8,128)(2,1)} %bitcast.7, bf16[576,1152]{1,0:T(8,128)(2,1)} %wos_hbm.1, bf16[108,1152]{1,0:T(8,128)(2,1)} %bitcast.10, ...), custom_call_target="tpu_custom_call" | custom-call | tf_op jit(solution)/shard_map/block/pallas_call | solution.py:529
  81.2 2.1 %finish.1 = (bf16[128,1152]{1,0:T(8,128)(2,1)}, bf16[128,1152]{1,0:T(8,128)(2,1)}, bf16[128,1728]{1,0:T(8,128)(2,1)}, f32[18,72]{1,0:T(8,128)}, f32[18,72]{1,0:T(8,128)}) custom-call(bf16[128,1152]{1,0:T(8,128)(2,1)} %get-tuple-element.14.block_hbm, bf16[128,1152]{1,0:T(8,128)(2,1)} %get-tuple-element.15.tgrad_hbm, ...), custom_call_target="tpu_custom_call" | custom-call | tf_op jit(solution)/shard_map/finish/pallas_call | solution.py:546

commit v6 on v5

--- a/solution.py
+++ b/solution.py
@@ -434,10 +434,10 @@
     tg_s[...] = total.astype(BF).reshape(8, 16, D)
     tg_swap = send(tg_s, tgx, oss.at[3], ors.at[3], partner)
     tokens_copies = exchange(3, tg_s, tg_r)
-    next(temporal_sum)
     arrived((tg_swap, spatial_left))
     next(spatial_sum)
     next(spatial_sum)
+    next(temporal_sum)
 
     arrived(out_copies)
     block[...] = (hid[...].astype(F32) + nn(from_peers(to_r).astype(BF), wot[...])).astype(BF)

time: 83.6 us -> 83.4 us (level)
  no operation moved by 1% of the time
where the time goes in v6:
time: 83.4 us; the launch traced here: 83.2 us
  Pallas kernels  82.4 us (99%)
    pallas_call x1, Pallas kernels, shards(): pl.pallas_call(kernel, out_shape=[jax.ShapeDtypeStruct((ROWS, D), BF), ja...  80.3 us
    pallas_call x1, Pallas kernels, shards(): pl.pallas_call(finish_kernel, out_shape=[jax.ShapeDtypeStruct((ROWS, D),...  2.06 us

profile of v6, /device:TPU:1, one launch (start us, length us, event | category | flops | bytes accessed | tf_op | source)
XLA Modules:
  0.0 83.2 jit_solution(13963853715356324634)
XLA Ops:
  0.6 80.3 %block.1 = (bf16[128,1152]{1,0:T(8,128)(2,1)}, bf16[128,1152]{1,0:T(8,128)(2,1)}, bf16[128,1728]{1,0:T(8,128)(2,1)}, f32[2,16,128]{2,1,0:T(8,128)}) custom-call(bf16[128,1152]{1,0:T(8,128)(2,1)} %bitcast.8, bf16[128,1728]{1,0:T(8,128)(2,1)} %bitcast.7, bf16[576,1152]{1,0:T(8,128)(2,1)} %wos_hbm.1, bf16[108,1152]{1,0:T(8,128)(2,1)} %bitcast.10, ...), custom_call_target="tpu_custom_call" | custom-call | tf_op jit(solution)/shard_map/block/pallas_call | solution.py:529
  80.9 2.1 %finish.1 = (bf16[128,1152]{1,0:T(8,128)(2,1)}, bf16[128,1152]{1,0:T(8,128)(2,1)}, bf16[128,1728]{1,0:T(8,128)(2,1)}, f32[18,72]{1,0:T(8,128)}, f32[18,72]{1,0:T(8,128)}) custom-call(bf16[128,1152]{1,0:T(8,128)(2,1)} %get-tuple-element.14.block_hbm, bf16[128,1152]{1,0:T(8,128)(2,1)} %get-tuple-element.15.tgrad_hbm, ...), custom_call_target="tpu_custom_call" | custom-call | tf_op jit(solution)/shard_map/finish/pallas_call | solution.py:546

commit v7 on v6

--- a/solution.py
+++ b/solution.py
@@ -401,7 +401,6 @@
     cot_swap = send(cot_r, cotx, oss.at[2], ors.at[2], partner)
     attend(tqkv, same_patch, pt_ref, to, range(8))
     to_s[...] = to[...].reshape(8, 16, HD)
-    out_copies = exchange(2, to_s, to_r)
     temporal_left = left_operand(1, to[...])
     og[...] = nt(cot_r[...].reshape(ROWS, D), wot[...]).astype(BF)
     arrived(spatial_copies)
@@ -437,23 +436,25 @@
     arrived((tg_swap, spatial_left))
     next(spatial_sum)
     next(spatial_sum)
+    out_copies = exchange(2, to_s, to_r)
     next(temporal_sum)
 
-    arrived(out_copies)
-    block[...] = (hid[...].astype(F32) + nn(from_peers(to_r).astype(BF), wot[...])).astype(BF)
-    outs = [pltpu.make_async_copy(block, block_hbm, out_sems.at[0])]
-    outs[0].start()
+    outs = []
     next(temporal_sum)
     arrived(tokens_copies)
     tgrad[...] = from_peers(tg_r).astype(BF)
     outs.append(pltpu.make_async_copy(tgrad, tgrad_hbm, out_sems.at[1]))
-    outs[1].start()
+    outs[0].start()
     sog[...] = nt(tgrad[...], wos[...]).astype(BF)
     next(spatial_sum)
     attend_grad(sqkv, ps_ref, sog, sgrad, range(0, 4))
     next(spatial_sum)
     attend_grad(sqkv, ps_ref, sog, sgrad, range(4, 8))
     outs.append(pltpu.make_async_copy(sgrad, sgrad_hbm, out_sems.at[2]))
+    outs[1].start()
+    arrived(out_copies)
+    block[...] = (hid[...].astype(F32) + nn(from_peers(to_r).astype(BF), wot[...])).astype(BF)
+    outs.append(pltpu.make_async_copy(block, block_hbm, out_sems.at[0]))
     outs[2].start()
     next(temporal_sum)
     next(spatial_sum)

time: 83.4 us -> 83.8 us (level)
  no operation moved by 1% of the time
where the time goes in v7:
time: 83.8 us; the launch traced here: 83.6 us
  Pallas kernels  82.8 us (99%)
    pallas_call x1, Pallas kernels, shards(): pl.pallas_call(kernel, out_shape=[jax.ShapeDtypeStruct((ROWS, D), BF), ja...  80.8 us
    pallas_call x1, Pallas kernels, shards(): pl.pallas_call(finish_kernel, out_shape=[jax.ShapeDtypeStruct((ROWS, D),...  2.06 us

profile of v7, /device:TPU:1, one launch (start us, length us, event | category | flops | bytes accessed | tf_op | source)
XLA Modules:
  0.0 83.6 jit_solution(8413533059000763112)
XLA Ops:
  0.6 80.8 %block.1 = (bf16[128,1152]{1,0:T(8,128)(2,1)}, bf16[128,1152]{1,0:T(8,128)(2,1)}, bf16[128,1728]{1,0:T(8,128)(2,1)}, f32[2,16,128]{2,1,0:T(8,128)}) custom-call(bf16[128,1152]{1,0:T(8,128)(2,1)} %bitcast.8, bf16[128,1728]{1,0:T(8,128)(2,1)} %bitcast.7, bf16[576,1152]{1,0:T(8,128)(2,1)} %wos_hbm.1, bf16[108,1152]{1,0:T(8,128)(2,1)} %bitcast.10, ...), custom_call_target="tpu_custom_call" | custom-call | tf_op jit(solution)/shard_map/block/pallas_call | solution.py:530
  81.4 2.1 %finish.1 = (bf16[128,1152]{1,0:T(8,128)(2,1)}, bf16[128,1152]{1,0:T(8,128)(2,1)}, bf16[128,1728]{1,0:T(8,128)(2,1)}, f32[18,72]{1,0:T(8,128)}, f32[18,72]{1,0:T(8,128)}) custom-call(bf16[128,1152]{1,0:T(8,128)(2,1)} %get-tuple-element.14.block_hbm, bf16[128,1152]{1,0:T(8,128)(2,1)} %get-tuple-element.15.tgrad_hbm, ...), custom_call_target="tpu_custom_call" | custom-call | tf_op jit(solution)/shard_map/finish/pallas_call | solution.py:547
